TPU v7x, 256 devices: a whole 4x4x8 slice. The times are simulated.
256 devices in a mesh: dp: 8 (over x, core), vocab: 32 (over y, z).
Axes of the slice: x: 4, y: 4, z: 8, core: 2. Of those that a mesh axis runs over, the one named last changes fastest.
Arguments:
- head_input: bfloat16 [1024, 8192], P(('dp', 'vocab')), may hold values from -250 to 250
- body_input: bfloat16 [1024, 8192], P(('dp', 'vocab')), may hold values from -6 to 6
- head_weight: bfloat16 [16384, 8192], P('vocab'), may hold values from -0.0625 to 0.0625
- gate_weight: bfloat16 [8192, 14336], P('dp', 'vocab'), may hold values from -0.0625 to 0.0625
- up_weight: bfloat16 [8192, 14336], P('dp', 'vocab'), may hold values from -0.0625 to 0.0625
- down_weight: bfloat16 [8192, 14336], P('dp', 'vocab'), may hold values from -0.046875 to 0.046875
- tile_ids: int32 [2048, 128], P(('dp', 'vocab')), may hold values from 0 to 16383, as said below
- tile_probs: bfloat16 [2048, 128], P(('dp', 'vocab')), may hold values from 0 to 1, as said below
- tile_slot: int32 [1024], P('dp'), may hold values from 0 to 255, as said below
Outputs:
- input_grad: bfloat16 [1024, 8192], P('dp', 'vocab')
Inputs may be any that keep to these rules, and one draw needn't show every extreme that they name: `tile_ids`: each stored slot lists 128 distinct token ids. `tile_probs`: in every slot the probabilities are positive and sum to at most 0.95. `tile_slot`: A group's store of 256 slots lies on the devices of one index of dp in order of vocab, 8 slots a device; rows of a group use distinct slots, so half of the slots hold no row's tile and are never read; in every group all 8 slots of some device are used, and which device varies.
All inputs are finite; a program needn't handle non-finite values.
Results may differ from a plain program's by a relative error of at most 0.02.
Values may be sent and summed in bfloat16 or wider, within the bound.
No kernel may reach another device: no remote copies, remote signals or barrier semaphores. Data moves between devices by JAX's collectives and lax.ppermute only.
A program may use at most 128 MiB of HBM per device.

v0:
```python
import jax
import jax.numpy as jnp
from jax import lax
from jax.sharding import PartitionSpec as P

MICRO = 2
MB_ROWS = 64
LOSS_SCALE = 1024


def merged(shard, axis, combine):
    everything = jax.tree.map(lambda part: lax.all_gather(part, axis), shard)
    leading = jax.tree.map(lambda part: part[0], everything)

    def hop(k, so_far):
        return combine(so_far, jax.tree.map(lambda part: part[k], everything))

    return lax.fori_loop(1, lax.axis_size(axis), hop, leading)


def combine_stats(earlier, later):
    first_max, first_top, first_rest_max, first_rest = earlier
    second_max, second_top, second_rest_max, second_rest = later
    joint_max = jnp.maximum(first_max, second_max)
    joint_top = first_top * jnp.exp(first_max - joint_max) + second_top * jnp.exp(
        second_max - joint_max
    )
    joint_rest_max = jnp.maximum(first_rest_max, second_rest_max)
    joint_rest = first_rest * jnp.exp(first_rest_max - joint_rest_max) + second_rest * jnp.exp(
        second_rest_max - joint_rest_max
    )
    return (joint_max, joint_top, joint_rest_max, joint_rest)


def swiglu_grads(gate_act, up_act, down_grad):
    sigma = jax.nn.sigmoid(gate_act)
    gate_grad = (down_grad * up_act * sigma * (1.0 + gate_act * (1.0 - sigma))).astype(jnp.bfloat16)
    up_grad = (down_grad * gate_act * sigma).astype(jnp.bfloat16)
    return (gate_grad, up_grad)


def body(
    head_input,
    body_input,
    head_weight,
    gate_weight,
    up_weight,
    down_weight,
    tile_ids,
    tile_probs,
    tile_slot,
):
    head_rows, body_rows, store_ids, store_probs = (
        lax.all_gather(head_input, "vocab", axis=0, tiled=True),
        lax.all_gather(body_input, "vocab", axis=0, tiled=True),
        lax.all_gather(tile_ids, "vocab", axis=0, tiled=True),
        lax.all_gather(tile_probs, "vocab", axis=0, tiled=True),
    )
    gate_full, up_full, down_full = (
        lax.all_gather(gate_weight, "dp", axis=0, tiled=True),
        lax.all_gather(up_weight, "dp", axis=0, tiled=True),
        lax.all_gather(down_weight, "dp", axis=0, tiled=True),
    )
    vocab_rows = head_weight.shape[0]
    place = lax.axis_index("vocab")
    shards = lax.axis_size("vocab")
    share = head_rows.shape[1] // shards
    row_ids = store_ids[tile_slot]
    row_probs = store_probs[tile_slot].astype(jnp.float32)
    tail_mass = 1.0 - jnp.sum(row_probs, axis=1, keepdims=True)
    columns = row_ids - place * vocab_rows
    inside = (columns >= 0) & (columns < vocab_rows)
    target = jnp.where(inside, columns, vocab_rows)
    count = row_ids.shape[0]
    lines = jnp.broadcast_to(jnp.arange(count, dtype=jnp.int32)[:, None], row_ids.shape)
    teacher = (
        jnp.zeros((count, vocab_rows), jnp.float32).at[lines, target].add(row_probs, mode="drop")
    )
    chosen = jnp.zeros((count, vocab_rows), jnp.bool_).at[lines, target].set(True, mode="drop")

    def handle(start, length):
        rows_head = head_rows[start : start + length]
        rows_body = body_rows[start : start + length]
        picked = chosen[start : start + length]
        target_probs = teacher[start : start + length]
        tail_part = tail_mass[start : start + length]
        logits = jnp.einsum("rd,vd->rv", rows_head, head_weight, preferred_element_type=jnp.float32)
        local_max = jnp.max(logits, axis=1, keepdims=True)
        rest = jnp.where(picked, -1e30, logits)
        local_rest_max = jnp.max(rest, axis=1, keepdims=True)
        local_top = jnp.sum(
            jnp.where(picked, jnp.exp(logits - local_max), 0.0), axis=1, keepdims=True
        )
        local_rest = jnp.sum(
            jnp.where(picked, 0.0, jnp.exp(rest - local_rest_max)), axis=1, keepdims=True
        )
        row_max, top_sum, rest_max, rest_sum = merged(
            (local_max, local_top, local_rest_max, local_rest), "vocab", combine_stats
        )
        total = top_sum + rest_sum * jnp.exp(rest_max - row_max)
        student = jnp.exp(logits - row_max) / total
        spread = jnp.where(picked, 0.0, jnp.exp(rest - rest_max)) / rest_sum
        top_share = top_sum / total
        logit_grad = (
            LOSS_SCALE
            * (
                student * (1.0 - tail_part)
                + jnp.where(
                    picked, tail_part * student - target_probs, -tail_part * top_share * spread
                )
            )
        ).astype(jnp.bfloat16)
        partial_grad = jnp.dot(logit_grad, head_weight, preferred_element_type=jnp.float32)
        head_full = lax.psum(partial_grad.astype(jnp.bfloat16), "vocab")
        head_own = lax.dynamic_slice_in_dim(head_full, place * share, share, 1)
        gate_act = jnp.dot(rows_body, gate_full, preferred_element_type=jnp.float32)
        up_act = jnp.dot(rows_body, up_full, preferred_element_type=jnp.float32)
        down_grad = jnp.dot(head_full, down_full, preferred_element_type=jnp.float32)
        gate_grad, up_grad = swiglu_grads(gate_act, up_act, down_grad)
        branch = jnp.einsum("rf,df->rd", gate_grad, gate_full, preferred_element_type=jnp.float32)
        branch = branch + jnp.einsum(
            "rf,df->rd", up_grad, up_full, preferred_element_type=jnp.float32
        )
        summed = lax.psum_scatter(
            branch.astype(jnp.bfloat16), "vocab", scatter_dimension=1, tiled=True
        ).astype(jnp.float32)
        return (head_own.astype(jnp.float32) + summed).astype(jnp.bfloat16)

    input_grad = jnp.concatenate(
        [handle(index * MB_ROWS, MB_ROWS) for index in range(MICRO)], axis=0
    )
    return input_grad


def solution(mesh):
    return jax.shard_map(
        body,
        mesh=mesh,
        in_specs=(
            P(("dp", "vocab"), None),
            P(("dp", "vocab"), None),
            P("vocab", None),
            P("dp", "vocab"),
            P("dp", "vocab"),
            P("dp", "vocab"),
            P(("dp", "vocab"), None),
            P(("dp", "vocab"), None),
            P("dp"),
        ),
        out_specs=P("dp", "vocab"),
        check_vma=False,
    )
```

profile of v0, /device:TPU:2, one launch (start us, length us, event | category | flops | bytes accessed | tf_op | source)
XLA Modules:
  0.0 1128.3 jit_solution(14669337983128712621)
XLA Ops:
  7.3 46.7 %all_gather.47 = s32[256,128]{1,0:T(8,128)S(1)} all-gather(s32[8,128]{1,0:T(8,128)} %param.19), channel_id=1, replica_groups=mesh['dp'=8,'vocab'=32] {'vocab'}, dimensions={0}, use_global_device_ids=true | all-gather | bytes 135168 | tf_op jit(solution)/shard_map/all_gather | solution.py:56
  56.9 68.8 %scatter_custom_fusion = pred[65536]{0:T(1024)(128)(4,1)S(1)} fusion(s32[16384]{0:T(1024)S(1)} %select_bitcast_fusion, pred[16384]{0:T(1024)(128)(4,1)S(1)} %broadcast.131, pred[]{:T(512)} %constant.96.clone.1), kind=kCustom, calls=%fused_computation.69 | custom fusion | bytes 65537
  130.8 6.1 fusion.60
  137.7 6.2 fusion.61
  147.2 47.9 %all_gather.51 = bf16[256,128]{1,0:T(8,128)(2,1)S(1)} all-gather(bf16[8,128]{1,0:T(8,128)(2,1)S(1)} %copy-done.9), channel_id=1, replica_groups=mesh['dp'=8,'vocab'=32] {'vocab'}, dimensions={0}, use_global_device_ids=true | all-gather | bytes 67584 | tf_op jit(solution)/shard_map/all_gather | solution.py:57
  195.9 86.1 %scatter_custom_fusion.1 = f32[65536]{0:T(1024)S(1)} fusion(s32[16384]{0:T(1024)S(1)} %select_bitcast_fusion, f32[16384]{0:T(1024)S(1)} %convert_bitcast_fusion, f32[]{:T(128)} %constant.101.clone.1), kind=kCustom, calls=%fused_computation.50 | custom fusion | flops 16384 | bytes 262148
  282.2 4.1 all-reduce.13.cloned.1.call-done
  298.4 6.1 convolution_convert_fusion.1
  304.5 6.1 convolution_convert_fusion
  312.6 53.7 %all-gather.24.cloned.1.call-done = bf16[32,4,8192]{2,1,0:T(4,128)(2,1)} async-done(((bf16[1,4,8192]{2,1,0:T(4,128)(2,1)}), bf16[32,4,8192]{2,1,0:T(4,128)(2,1)}) %all-gather.24.cloned.1.call-update) | async-done | bytes 2097168 | tf_op jit(solution)/shard_map/all_gather | solution.py:55
  369.2 152.0 %all-reduce.15.cloned.1.call-done = (bf16[64,8192]{1,0:T(8,128)(2,1)}, bf16[64,8192]{1,0:T(8,128)(2,1)}) async-done(((bf16[64,8192]{1,0:T(8,128)(2,1)}, bf16[64,8192]{1,0:T(8,128)(2,1)}), (bf16[64,8192]{1,0:T(8,128)(2,1)}, bf16[64,8192]{1,0:T(8,128)(2,1)})) %all-reduce.15.cloned.1.call-update) | async-done | bytes 2097168 | tf_op jit(solution)/shard_map/psum | solution.py:114
  521.2 46.0 %all-gather.16.cloned.1.call-done = bf16[8192,448]{0,1:T(8,128)(2,1)} async-done(((bf16[1024,448]{0,1:T(8,128)(2,1)}), bf16[8192,448]{0,1:T(8,128)(2,1)}) %all-gather.16.cloned.1.call-update) | async-done | bytes 7340048 | tf_op jit(solution)/shard_map/all_gather | solution.py:62
  567.2 5.6 fusion.85
  572.9 44.0 %all-gather.20.cloned.1.call-done = bf16[8192,448]{0,1:T(8,128)(2,1)} async-done(((bf16[1024,448]{0,1:T(8,128)(2,1)}), bf16[8192,448]{0,1:T(8,128)(2,1)}) %all-gather.20.cloned.1.call-update) | async-done | bytes 7340048 | tf_op jit(solution)/shard_map/all_gather | solution.py:60
  616.9 5.3 fusion.86
  622.2 44.5 %all-gather.18.cloned.1.call-done = bf16[8192,448]{0,1:T(8,128)(2,1)} async-done(((bf16[1024,448]{0,1:T(8,128)(2,1)}), bf16[8192,448]{0,1:T(8,128)(2,1)}) %all-gather.18.cloned.1.call-update) | async-done | bytes 7340048 | tf_op jit(solution)/shard_map/all_gather | solution.py:61
  666.7 10.5 fusion.29
  677.2 6.1 fusion.20
  683.7 5.3 fusion.87
  689.0 5.3 fusion.88
  694.3 9.2 fusion.28
  703.5 5.5 fusion.21
  709.0 192.4 %reduce-scatter.3.cloned.1.call-done = bf16[64,256]{1,0:T(8,128)(2,1)} async-done(((bf16[64,8192]{1,0:T(8,128)(2,1)}), bf16[64,256]{1,0:T(8,128)(2,1)}) %reduce-scatter.3.cloned.1.call-update) | async-done | bytes 32784 | tf_op jit(solution)/shard_map/reduce_scatter | solution.py:124
  902.2 218.1 %reduce-scatter.5.cloned.1.call-done = bf16[64,256]{1,0:T(8,128)(2,1)} async-done(((bf16[64,8192]{1,0:T(8,128)(2,1)}), bf16[64,256]{1,0:T(8,128)(2,1)}) %reduce-scatter.5.cloned.1.call-update) | async-done | bytes 32784 | tf_op jit(solution)/shard_map/reduce_scatter | solution.py:124
  (164 shorter events, 34.1 us)
Async XLA Ops:
  6.5 121.3 %all-gather.22.cloned.1.call-start = ((), (), s32[]{:S(2)}) async-start(), calls=%async_computation.7 | async-start | bytes 2162688 | tf_op jit(solution)/shard_map/all_gather | solution.py:54
  7.3 279.0 %all-reduce.13.cloned.1.call-start = ((), (), s32[]{:S(2)}) async-start(), calls=%async_computation.9 | async-start | bytes 131072
  136.9 10.2 copy-start.9
  137.5 8.3 copy-start.2
  137.7 8.0 copy-start.3
  144.2 1.6 copy-start.8
  144.7 1.1 copy-start.4
  144.9 0.8 copy-start.5
  145.2 0.6 copy-start.6
  145.5 0.6 copy-start.7
  145.7 0.6 copy-start.1
  146.4 219.9 %all-gather.24.cloned.1.call-start = ((), (), s32[]{:S(2)}) async-start(), calls=%async_computation.8 | async-start | bytes 2162688 | tf_op jit(solution)/shard_map/all_gather | solution.py:55
  147.1 374.1 %all-reduce.15.cloned.1.call-start = ((), (), s32[]{:S(2)}) async-start(), calls=%async_computation.10 | async-start | bytes 4194304 | tf_op jit(solution)/shard_map/psum | solution.py:114
  310.6 256.6 %all-gather.16.cloned.1.call-start = ((), (), s32[]{:S(2)}) async-start(), calls=%async_computation.2 | async-start | bytes 8257536 | tf_op jit(solution)/shard_map/all_gather | solution.py:62
  311.2 305.7 %all-gather.20.cloned.1.call-start = ((), (), s32[]{:S(2)}) async-start(), calls=%async_computation.4 | async-start | bytes 8257536 | tf_op jit(solution)/shard_map/all_gather | solution.py:60
  311.8 354.9 %all-gather.18.cloned.1.call-start = ((), (), s32[]{:S(2)}) async-start(), calls=%async_computation.3 | async-start | bytes 8257536 | tf_op jit(solution)/shard_map/all_gather | solution.py:61
  312.5 588.8 %reduce-scatter.3.cloned.1.call-start = ((), (), s32[]{:S(2)}) async-start(), calls=%async_computation.5 | async-start | bytes 1081344 | tf_op jit(solution)/shard_map/reduce_scatter | solution.py:124
  677.2 6.4 copy-start
  683.3 437.0 %reduce-scatter.5.cloned.1.call-start = ((), (), s32[]{:S(2)}) async-start(), calls=%async_computation.6 | async-start | bytes 1081344 | tf_op jit(solution)/shard_map/reduce_scatter | solution.py:124
Sparse Core Ops, SparseCore 0:
  9.9 81.0 all-gather.21
  146.5 139.7 all-reduce.12
  288.9 77.3 all-gather.23
  369.8 151.3 all-reduce.14
  522.9 44.3 all-gather.15
  568.9 47.9 all-gather.19
  618.7 47.9 all-gather.17
  683.5 217.8 reduce-scatter.2
  905.2 215.0 reduce-scatter.4
where the time goes:
time: 1130 us
  waiting for transfers between devices  758 us (67%)
  blocking collectives  94.6 us (8%)
  other arithmetic  92.9 us (8%)
  local copies, waits for them, and re-layouts  89.3 us (8%)
  matrix products  77.3 us (7%)
  between operations  14.2 us (1%)
    reduce_scatter x2, waiting for transfers between devices, handle(): lax.psum_scatter(branch.astype(jnp.bfloat16), 'vocab', scatter_dimension=...  411 us
    psum x1, waiting for transfers between devices, handle(): head_full = lax.psum(partial_grad.astype(jnp.bfloat16), 'vocab')  152 us
    unnamed x4, other arithmetic  87.6 us
    unnamed x39, local copies, waits for them, and re-layouts  72.9 us
    all_gather x1, waiting for transfers between devices, body(): lax.all_gather(body_input, 'vocab', axis=0, tiled=True)  53.7 us
    all_gather x1, blocking collectives, body(): lax.all_gather(tile_probs, 'vocab', axis=0, tiled=True)  47.9 us
    all_gather x1, blocking collectives, body(): lax.all_gather(tile_ids, 'vocab', axis=0, tiled=True)  46.7 us
    all_gather x1, waiting for transfers between devices, body(): lax.all_gather(down_weight, 'dp', axis=0, tiled=True)  46 us
  transfers between devices with their start and end apart: 9, of which 8 were waited for; matrix products, arithmetic and copies ran while one was open for 20% of the time, Pallas kernels for 0%

commit v1 on v0

v1 whole, which is shorter than its diff:
```python
import jax
import jax.numpy as jnp
from jax import lax
from jax.experimental import pallas as pl
from jax.sharding import PartitionSpec as P


LOSS_SCALE = 1024
NX, NY, NZ, CORES = 4, 4, 8, 2
RADIX = 128

Y_GROUPS = [[y * NZ + z for y in range(NY)] for z in range(NZ)]
Z_GROUPS = [[y * NZ + z for z in range(NZ)] for y in range(NY)]
SWAP_XY = [
    (
        (x * CORES + c) * NY * NZ + y * NZ + z,
        (y * CORES + c) * NY * NZ + x * NZ + z,
    )
    for x in range(NX)
    for c in range(CORES)
    for y in range(NY)
    for z in range(NZ)
]
NT = (((1,), (1,)), ((), ()))


def exchange(blocks, groups=None):
    return lax.all_to_all(blocks, "vocab", 0, 0, axis_index_groups=groups)


def replicate(block, copies):
    return jnp.broadcast_to(block[None], (copies,) + block.shape)


def as_tiles(rows):
    count, width = rows.shape
    return rows.reshape(count, width // 128, 128).transpose(1, 0, 2).reshape(-1, 128)


def from_tiles(blocks, rows):
    shards, size, lanes = blocks.shape
    blocks = blocks.reshape(shards, size // rows, rows, lanes).transpose(0, 2, 1, 3)
    return blocks.reshape(shards * rows, size // rows * lanes)


def add_blocks(blocks):
    return jnp.sum(blocks.astype(jnp.float32), axis=0)


def wide_kernel(rows_ref, weight_ref, out_ref):
    half = weight_ref.shape[2]
    total = lax.dot_general(
        rows_ref[:, :half], weight_ref[0], NT, preferred_element_type=jnp.float32
    )
    total += lax.dot_general(
        rows_ref[:, half:], weight_ref[1], NT, preferred_element_type=jnp.float32
    )
    out_ref[0] = total.astype(out_ref.dtype)


def wide(rows, weight):
    count = rows.shape[0]
    blocks, hidden, half = weight.shape
    parts = blocks // CORES
    return pl.pallas_call(
        wide_kernel,
        grid=(parts,),
        in_specs=[
            pl.BlockSpec(rows.shape, lambda i: (0, 0)),
            pl.BlockSpec((CORES, hidden, half), lambda i: (i, 0, 0)),
        ],
        out_specs=pl.BlockSpec((1, count, hidden), lambda i: (i, 0, 0)),
        out_shape=jax.ShapeDtypeStruct((parts, count, hidden), jnp.bfloat16),
        cost_estimate=pl.CostEstimate(
            flops=2 * count * blocks * hidden * half,
            bytes_accessed=2 * (weight.size + rows.size),
            transcendentals=0,
        ),
        name="wide",
    )(rows, weight)


def branch_kernel(gate_ref, up_ref, gate_weight_ref, up_weight_ref, out_ref):
    total = None
    for i in range(gate_ref.shape[0]):
        for act, weight in ((gate_ref, gate_weight_ref), (up_ref, up_weight_ref)):
            part = jnp.dot(act[i], weight[i, 0], preferred_element_type=jnp.float32)
            total = part if total is None else total + part
    out_ref[0] = total.astype(out_ref.dtype)


def branch_blocks(gate, up, gate_weight, up_weight):
    parts, count, hidden = gate.shape
    half = gate_weight.shape[2]
    share = CORES * half // NZ
    per = half // share
    gate_weight = gate_weight.reshape(parts, CORES, hidden, half)
    up_weight = up_weight.reshape(parts, CORES, hidden, half)
    weight_spec = pl.BlockSpec((parts, 1, hidden, share), lambda i: (0, i // per, 0, i % per))
    act_spec = pl.BlockSpec(gate.shape, lambda i: (0, 0, 0))
    return pl.pallas_call(
        branch_kernel,
        grid=(NZ,),
        in_specs=[act_spec, act_spec, weight_spec, weight_spec],
        out_specs=pl.BlockSpec((1, count, share), lambda i: (i, 0, 0)),
        out_shape=jax.ShapeDtypeStruct((NZ, count, share), jnp.bfloat16),
        cost_estimate=pl.CostEstimate(
            flops=4 * count * gate_weight.size,
            bytes_accessed=4 * gate_weight.size,
            transcendentals=0,
        ),
        name="branch",
    )(gate, up, gate_weight, up_weight)


def head_kernel(grad_ref, weight_ref, out_ref):
    for i in range(out_ref.shape[0]):
        share = out_ref.shape[2]
        out_ref[i] = jnp.dot(
            grad_ref[...],
            weight_ref[:, i * share : (i + 1) * share],
            preferred_element_type=jnp.float32,
        ).astype(out_ref.dtype)


def head_blocks(grad, weight):
    count, vocab = grad.shape
    width = weight.shape[1]
    parts = NY * NZ
    share = width // parts
    step = 4
    return pl.pallas_call(
        head_kernel,
        grid=(parts // step,),
        in_specs=[
            pl.BlockSpec(grad.shape, lambda i: (0, 0)),
            pl.BlockSpec((vocab, step * share), lambda i: (0, i)),
        ],
        out_specs=pl.BlockSpec((step, count, share), lambda i: (i, 0, 0)),
        out_shape=jax.ShapeDtypeStruct((parts, count, share), jnp.bfloat16),
        cost_estimate=pl.CostEstimate(
            flops=2 * count * weight.size,
            bytes_accessed=2 * weight.size,
            transcendentals=0,
        ),
        name="head",
    )(grad, weight)


def marks_kernel(columns_ref, probs_ref, out_ref):
    _, entries = columns_ref.shape
    lanes = lax.broadcasted_iota(jnp.int32, out_ref.shape, 1)
    columns = columns_ref[...]
    probs = probs_ref[...]
    marks = jnp.full(out_ref.shape, -1.0, jnp.float32)
    for k in range(entries):
        marks = jnp.where(lanes == columns[:, k : k + 1], probs[:, k : k + 1], marks)
    out_ref[...] = marks


def make_marks(columns, probs, vocab):
    count, entries = columns.shape
    step = 16
    spec = pl.BlockSpec((step, entries), lambda i: (i, 0))
    return pl.pallas_call(
        marks_kernel,
        grid=(count // step,),
        in_specs=[spec, spec],
        out_specs=pl.BlockSpec((step, vocab), lambda i: (i, 0)),
        out_shape=jax.ShapeDtypeStruct((count, vocab), jnp.float32),
        cost_estimate=pl.CostEstimate(
            flops=2 * count * entries * vocab, bytes_accessed=4 * count * vocab, transcendentals=0
        ),
        name="marks",
    )(columns, probs)


def land_kernel(moved_ref, out_ref):
    out_ref[...] = moved_ref[...]


def gather_weight(weight):
    moved = lax.ppermute(weight.T, ("dp", "vocab"), SWAP_XY)
    hidden, half = moved.shape
    step = hidden // 4
    spec = pl.BlockSpec((step, half), lambda i: (i, 0))
    landed = pl.pallas_call(
        land_kernel,
        grid=(4,),
        in_specs=[spec],
        out_specs=spec,
        out_shape=jax.ShapeDtypeStruct(moved.shape, moved.dtype),
        cost_estimate=pl.CostEstimate(flops=0, bytes_accessed=4 * moved.size, transcendentals=0),
        name="land",
    )(moved)
    return lax.all_gather(landed, "dp", axis=0)


def layers(
    head_input,
    body_input,
    head_weight,
    gate_weight,
    up_weight,
    down_weight,
    tile_ids,
    tile_probs,
    tile_slot,
):
    shards = NY * NZ
    own_rows, width = head_input.shape
    slots, entries = tile_ids.shape
    vocab = head_weight.shape[0]
    count = shards * own_rows
    place = lax.axis_index("vocab")
    share = width // shards

    gate_full = gather_weight(gate_weight)
    up_full = gather_weight(up_weight)
    down_full = gather_weight(down_weight)

    tiles = width // 128
    quarter = width // NY
    shared = jnp.concatenate(
        [
            as_tiles(head_input),
            (tile_ids // RADIX).astype(jnp.bfloat16).reshape(-1, 128),
            (tile_ids % RADIX).astype(jnp.bfloat16).reshape(-1, 128),
            tile_probs.reshape(-1, 128),
        ],
        axis=0,
    )
    size = own_rows * tiles
    packed = jnp.concatenate(
        [replicate(shared, NY), as_tiles(body_input).reshape(NY, -1, 128)], axis=1
    )
    packed = jnp.broadcast_to(packed[:, None], (NY, NZ) + packed.shape[1:])
    packed = packed.reshape((shards,) + packed.shape[2:])
    arrived = exchange(packed)
    head_rows = from_tiles(arrived[:, :size], own_rows)
    body_rows = from_tiles(arrived[:, shared.shape[0] :], own_rows)
    store = (
        arrived[:, size : shared.shape[0]]
        .reshape(shards, 3, slots, entries)
        .transpose(0, 2, 1, 3)
        .reshape(shards * slots, 3 * entries)
    )
    chosen_slot = (
        tile_slot[:, None] == lax.broadcasted_iota(jnp.int32, (count, shards * slots), 1)
    ).astype(jnp.bfloat16)
    found = jnp.dot(chosen_slot, store, preferred_element_type=jnp.float32)
    row_ids = (found[:, :entries] * RADIX + found[:, entries : 2 * entries]).astype(jnp.int32)
    row_probs = found[:, 2 * entries :]
    tail_mass = 1.0 - jnp.sum(row_probs, axis=1, keepdims=True)
    marks = make_marks(row_ids - place * vocab, row_probs, vocab)
    picked = marks >= 0.0
    teacher = jnp.maximum(marks, 0.0)

    logits = jnp.einsum("rd,vd->rv", head_rows, head_weight, preferred_element_type=jnp.float32)
    local_max = jnp.max(logits, axis=1, keepdims=True)
    rest = jnp.where(picked, -1e30, logits)
    local_rest_max = jnp.max(rest, axis=1, keepdims=True)
    local_top = jnp.sum(jnp.where(picked, jnp.exp(logits - local_max), 0.0), axis=1, keepdims=True)
    local_rest = jnp.sum(
        jnp.where(picked, 0.0, jnp.exp(rest - local_rest_max)), axis=1, keepdims=True
    )
    stats = jnp.concatenate([local_max, local_rest_max, local_top, local_rest], axis=1).T
    maxima, rest_maxima, tops, rests = jnp.split(exchange(replicate(stats, shards)), 4, axis=1)
    row_max = jnp.max(maxima, axis=0)
    rest_max = jnp.max(rest_maxima, axis=0)
    top_sum = jnp.sum(tops * jnp.exp(maxima - row_max), axis=0)
    rest_sum = jnp.sum(rests * jnp.exp(rest_maxima - rest_max), axis=0)
    total = top_sum + rest_sum * jnp.exp(rest_max - row_max)
    row_max, rest_max, rest_sum, total, top_share = (
        value.reshape(count, 1) for value in (row_max, rest_max, rest_sum, total, top_sum / total)
    )
    student = jnp.exp(logits - row_max) / total
    spread = jnp.where(picked, 0.0, jnp.exp(rest - rest_max)) / rest_sum
    logit_grad = (
        LOSS_SCALE
        * (
            student * (1.0 - tail_mass)
            + jnp.where(picked, tail_mass * student - teacher, -tail_mass * top_share * spread)
        )
    ).astype(jnp.bfloat16)

    gate_part = wide(body_rows, gate_full)
    up_part = wide(body_rows, up_full)

    partial = head_blocks(logit_grad, head_weight).reshape(NY, NZ, count, share)
    over_y = add_blocks(exchange(partial, Y_GROUPS)).astype(jnp.bfloat16)
    head_own = add_blocks(exchange(over_y, Z_GROUPS)).astype(jnp.bfloat16)
    head_grad = (
        exchange(replicate(head_own, NZ), Z_GROUPS).transpose(1, 0, 2).reshape(count, quarter)
    )

    parts = jnp.stack([gate_part, up_part, wide(head_grad, down_full)], axis=1)
    gate_act, up_act, down_grad = add_blocks(exchange(parts, Y_GROUPS))
    sigma = 1.0 / (1.0 + jnp.exp(-gate_act))
    gate_grad = (down_grad * up_act * sigma * (1.0 + gate_act * (1.0 - sigma))).astype(jnp.bfloat16)
    up_grad = (down_grad * gate_act * sigma).astype(jnp.bfloat16)
    both = exchange(replicate(jnp.stack([gate_grad, up_grad]), NY), Y_GROUPS)
    pieces = branch_blocks(both[:, 0], both[:, 1], gate_full, up_full)
    summed = add_blocks(exchange(pieces, Z_GROUPS))
    return (head_own.astype(jnp.float32) + summed).astype(jnp.bfloat16)


def solution(mesh):
    return jax.shard_map(
        layers,
        mesh=mesh,
        in_specs=(
            P(("dp", "vocab"), None),
            P(("dp", "vocab"), None),
            P("vocab", None),
            P("dp", "vocab"),
            P("dp", "vocab"),
            P("dp", "vocab"),
            P(("dp", "vocab"), None),
            P(("dp", "vocab"), None),
            P("dp"),
        ),
        out_specs=P("dp", "vocab"),
        check_vma=False,
    )
```

time: 1130 us -> 455 us (0.40)
  waiting for transfers between devices: 758 us -> 202 us
  other arithmetic: 92.9 us -> 7.85 us
  local copies, waits for them, and re-layouts: 89.3 us -> 13.5 us
  matrix products: 77.3 us -> 7.53 us
  Pallas kernels: 0 us -> 55 us
  starting transfers between devices: 0.58 us -> 46.5 us
  blocking collectives: 94.6 us -> 108 us
    reduce_scatter x2 -> x0, waiting for transfers between devices: 411 us -> none  [handle(): lax.psum_scatter(branch.astype(jnp.bfloat16), 'vocab', scatter_dimension=...]
    all_gather x5 -> x3, waiting for transfers between devices: 188 us -> 0.01 us  [gather_weight(): return lax.all_gather(landed, 'dp', axis=0)]
    psum x1 -> x0, waiting for transfers between devices: 152 us -> none  [handle(): head_full = lax.psum(partial_grad.astype(jnp.bfloat16), 'vocab')]
    ppermute x0 -> x3, waiting for transfers between devices: none -> 122 us  [gather_weight(): moved = lax.ppermute(weight.T, ('dp', 'vocab'), SWAP_XY)]
    all_to_all x0 -> x6, blocking collectives: none -> 108 us  [exchange(): return lax.all_to_all(blocks, 'vocab', 0, 0, axis_index_groups=groups)]
    all_gather x2 -> x0, blocking collectives: 94.6 us -> none  [the longest x1 47.9 us: body(): lax.all_gather(tile_probs, 'vocab', axis=0, tiled=True)]
    unnamed x4 -> x0, other arithmetic: 87.6 us -> none
    all_to_all x0 -> x2, waiting for transfers between devices: none -> 79.9 us  [exchange(): return lax.all_to_all(blocks, 'vocab', 0, 0, axis_index_groups=groups)]
  transfers between devices with their start and end apart: 9 -> 8, of which waited for: 8 -> 5; matrix products, arithmetic and copies ran while one was open for 20% -> 5% of each run, Pallas kernels for 0% -> 8%
where the time goes in v1:
time: 455 us; the launch traced here: 454 us
  waiting for transfers between devices  202 us (44%)
  blocking collectives  108 us (24%)
  Pallas kernels  55 us (12%)
  starting transfers between devices  46.5 us (10%)
  local copies, waits for them, and re-layouts  13.5 us (3%)
  between operations  13.4 us (3%)
  other arithmetic  7.85 us (2%)
  matrix products  7.53 us (2%)
    ppermute x3, waiting for transfers between devices, gather_weight(): moved = lax.ppermute(weight.T, ('dp', 'vocab'), SWAP_XY)  122 us
    all_to_all x6, blocking collectives, exchange(): return lax.all_to_all(blocks, 'vocab', 0, 0, axis_index_groups=groups)  108 us
    all_to_all x2, waiting for transfers between devices, exchange(): return lax.all_to_all(blocks, 'vocab', 0, 0, axis_index_groups=groups)  79.9 us
    all_to_all x2, starting transfers between devices, exchange(): return lax.all_to_all(blocks, 'vocab', 0, 0, axis_index_groups=groups)  34 us
    pallas_call x3, Pallas kernels, wide(): pl.pallas_call(wide_kernel, grid=(parts,), in_specs=[pl.BlockSpec(rows.sh...  18.1 us
    ppermute x3, starting transfers between devices, gather_weight(): moved = lax.ppermute(weight.T, ('dp', 'vocab'), SWAP_XY)  12.5 us
    pallas_call x3, Pallas kernels, gather_weight(): pl.pallas_call(land_kernel, grid=(4,), in_specs=[spec], out_specs=spec, o...  9.94 us
    pallas_call x1, Pallas kernels, branch_blocks(): pl.pallas_call(branch_kernel, grid=(NZ,), in_specs=[act_spec, act_spec, w...  9.81 us
  transfers between devices with their start and end apart: 8, of which 5 were waited for; matrix products, arithmetic and copies ran while one was open for 5% of the time, Pallas kernels for 8%

profile of v1, /device:TPU:2, one launch (start us, length us, event | category | flops | bytes accessed | tf_op | source)
XLA Modules:
  0.0 453.5 jit_solution(16833317053803884833)
XLA Ops:
  6.5 3.6 collective-permute-start
  10.1 41.3 %collective-permute-done.moved_ref = bf16[448,1024]{1,0:T(8,128)(2,1)S(1)} collective-permute-done((bf16[448,1024]{1,0:T(8,128)(2,1)}, bf16[448,1024]{1,0:T(8,128)(2,1)S(1)}, u32[]{:S(2)}, u32[]{:S(2)}) %collective-permute-start) | collective-permute-done | bytes 917536 | tf_op jit(solution)/shard_map/ppermute | solution.py:183
  55.7 3.6 collective-permute-start.1
  59.3 43.7 %collective-permute-done.1.moved_ref = bf16[448,1024]{1,0:T(8,128)(2,1)S(1)} collective-permute-done((bf16[448,1024]{1,0:T(8,128)(2,1)S(1)}, bf16[448,1024]{1,0:T(8,128)(2,1)S(1)}, u32[]{:S(2)}, u32[]{:S(2)}) %collective-permute-start.1) | collective-permute-done | bytes 917536 | tf_op jit(solution)/shard_map/ppermute | solution.py:183
  104.0 3.3 land.4
  107.4 5.3 %collective-permute-start.2 = (bf16[448,1024]{1,0:T(8,128)(2,1)S(1)}, bf16[448,1024]{1,0:T(8,128)(2,1)S(1)}, u32[]{:S(2)}, u32[]{:S(2)}) collective-permute-start(bf16[448,1024]{1,0:T(8,128)(2,1)S(1)} %bitcast.97), channel_id=1, source_target_pairs={{0,0},{1,1},{2,2},{3,3},{4,4},{5,5},{6,6},{7,7},{8,64},{9,65},{10,... | collective-permute-start | bytes 2752520 | tf_op jit(solution)/shard_map/ppermute | solution.py:183
  112.7 36.7 %collective-permute-done.2.moved_ref = bf16[448,1024]{1,0:T(8,128)(2,1)S(1)} collective-permute-done((bf16[448,1024]{1,0:T(8,128)(2,1)S(1)}, bf16[448,1024]{1,0:T(8,128)(2,1)S(1)}, u32[]{:S(2)}, u32[]{:S(2)}) %collective-permute-start.2) | collective-permute-done | bytes 917536 | tf_op jit(solution)/shard_map/ppermute | solution.py:183
  155.7 30.5 %all-to-all-start = ((bf16[32,344,128]{2,1,0:T(8,128)(2,1)}), bf16[32,344,128]{2,1,0:T(8,128)(2,1)S(1)}, u32[]{:S(2)}, u32[]{:S(2)}) async-start(bf16[32,344,128]{2,1,0:T(8,128)(2,1)} %bitcast.67), calls=%async_computation | async-start | bytes 5636096 | tf_op jit(solution)/shard_map/all_to_all | solution.py:28
  186.2 67.6 %all-to-all-done = bf16[32,344,128]{2,1,0:T(8,128)(2,1)S(1)} async-done(((bf16[32,344,128]{2,1,0:T(8,128)(2,1)}), bf16[32,344,128]{2,1,0:T(8,128)(2,1)S(1)}, u32[]{:S(2)}, u32[]{:S(2)}) %all-to-all-start) | async-done | bytes 2818080 | tf_op jit(solution)/shard_map/all_to_all | solution.py:28
  257.5 9.1 %marks.1 = f32[128,512]{1,0:T(8,128)} custom-call(s32[128,128]{1,0:T(8,128)} %fusion.9.columns_ref, f32[128,128]{1,0:T(8,128)} %get-tuple-element.17.probs_ref), custom_call_target="tpu_custom_call" | custom-call | flops 16777216 | bytes 262144 | tf_op jit(solution)/shard_map/marks/pallas_call | solution.py:165
  266.6 7.3 %fusion.15 = (f32[128]{0:T(128)S(1)}, f32[128]{0:T(128)S(1)}, pred[128,512]{1,0:T(8,128)(4,1)S(1)}, f32[128,512]{1,0:T(8,128)S(1)}) fusion(f32[128,512]{1,0:T(8,128)} %marks.1, bf16[512,8192]{1,0:T(8,128)(2,1)} %weight_ref.1, bf16[16,8,64,128]{3,2,1,0:T(8,128)(2,1)} %bitcast.69), kind=kOutput, calls=%fused_computation.49 | convolution fusion | flops 1074003712 | bytes 11076608 | tf_op jit(solution)/shard_map/rd,vd->rv/dot_general | solution.py:259
  274.2 14.1 %all_to_all.40 = f32[32,4,128]{2,1,0:T(4,128)S(1)} all-to-all(f32[32,4,128]{2,1,0:T(4,128)S(1)} %broadcast_in_dim.61), channel_id=1, replica_groups=mesh['dp'=8,'vocab'=32] {'vocab'}, dimensions={0} | all-to-all | bytes 131072 | tf_op jit(solution)/shard_map/all_to_all | solution.py:28
  289.4 8.1 %head.1 = bf16[32,128,256]{2,1,0:T(8,128)(2,1)} custom-call(bf16[128,512]{1,0:T(8,128)(2,1)} %multiply_convert_fusion.grad_ref, bf16[512,8192]{1,0:T(8,128)(2,1)} %weight_ref.1), custom_call_target="tpu_custom_call" | custom-call | flops 1073741824 | bytes 8388608 | tf_op jit(solution)/shard_map/head/pallas_call | solution.py:132
  297.5 29.4 %all_to_all.41 = bf16[4,8,128,256]{3,2,1,0:T(8,128)(2,1)} all-to-all(bf16[4,8,128,256]{3,2,1,0:T(8,128)(2,1)} %bitcast.70), channel_id=1, replica_groups={{0,8,16,24},{1,9,17,25},{2,10,18,26},{3,11,19,27},{4,12,20,28},{5,13,21..., dimensions={0} | all-to-all | bytes 4194304 | tf_op jit(solution)/shard_map/all_to_all | solution.py:28
  329.7 18.6 %all_to_all.42 = bf16[8,128,256]{2,1,0:T(8,128)(2,1)S(1)} all-to-all(bf16[8,128,256]{2,1,0:T(8,128)(2,1)} %reduce_sum.92), channel_id=1, replica_groups={{0,1,2,3,4,5,6,7},{8,9,10,11,12,13,14,15},{16,17,18,19,20,21,22,23},{24..., dimensions={0} | all-to-all | bytes 1048576 | tf_op jit(solution)/shard_map/all_to_all | solution.py:28
  349.2 3.5 all-to-all-start.4
  354.4 12.3 %all-to-all-done.4 = bf16[8,128,256]{2,1,0:T(8,128)(2,1)S(1)} async-done(((bf16[8,128,256]{2,1,0:T(8,128)(2,1)}), bf16[8,128,256]{2,1,0:T(8,128)(2,1)S(1)}, u32[]{:S(2)}, u32[]{:S(2)}) %all-to-all-start.4) | async-done | bytes 524320 | tf_op jit(solution)/shard_map/all_to_all | solution.py:28
  367.6 6.0 %wide.3 = bf16[4,128,448]{2,1,0:T(8,128)(2,1)} custom-call(bf16[128,2048]{1,0:T(8,128)(2,1)} %bitcast.72, bf16[8,448,1024]{2,1,0:T(8,128)(2,1)} %bitcast.63), custom_call_target="tpu_custom_call" | custom-call | flops 939524096 | bytes 7864320 | tf_op jit(solution)/shard_map/wide/pallas_call | solution.py:65
  373.6 6.0 %wide.4 = bf16[4,128,448]{2,1,0:T(8,128)(2,1)} custom-call(bf16[128,2048]{1,0:T(8,128)(2,1)} %bitcast.73, bf16[8,448,1024]{2,1,0:T(8,128)(2,1)} %bitcast.65), custom_call_target="tpu_custom_call" | custom-call | flops 939524096 | bytes 7864320 | tf_op jit(solution)/shard_map/wide/pallas_call | solution.py:65
  379.6 6.1 %wide.5 = bf16[4,128,448]{2,1,0:T(8,128)(2,1)} custom-call(bf16[128,2048]{1,0:T(8,128)(2,1)} %bitcast.74, bf16[8,448,1024]{2,1,0:T(8,128)(2,1)} %bitcast.71), custom_call_target="tpu_custom_call" | custom-call | flops 939524096 | bytes 7864320 | tf_op jit(solution)/shard_map/wide/pallas_call | solution.py:65
  387.8 15.4 %all_to_all.43 = bf16[4,3,128,448]{2,3,1,0:T(8,128)(2,1)S(1)} all-to-all(bf16[4,3,128,448]{2,3,1,0:T(8,128)(2,1)S(1)} %copy.62), channel_id=1, replica_groups={{0,8,16,24},{1,9,17,25},{2,10,18,26},{3,11,19,27},{4,12,20,28},{5,13,21..., dimensions={0} | all-to-all | bytes 2752512 | tf_op jit(solution)/shard_map/all_to_all | solution.py:28
  403.7 12.6 %all_to_all.44 = bf16[4,2,128,448]{2,3,1,0:T(8,128)(2,1)S(1)} all-to-all(bf16[4,2,128,448]{2,3,1,0:T(8,128)(2,1)S(1)} %broadcast_in_dim.63), channel_id=1, replica_groups={{0,8,16,24},{1,9,17,25},{2,10,18,26},{3,11,19,27},{4,12,20,28},{5,13,21..., dimensions={0} | all-to-all | bytes 1835008 | tf_op jit(solution)/shard_map/all_to_all | solution.py:28
  418.4 9.8 %branch.1 = bf16[8,128,256]{2,1,0:T(8,128)(2,1)} custom-call(bf16[4,128,448]{2,1,0:T(8,128)(2,1)} %bitcast.75, bf16[4,128,448]{2,1,0:T(8,128)(2,1)} %bitcast.76, bf16[4,2,448,1024]{3,2,1,0:T(8,128)(2,1)} %bitcast.64, bf16[4,2,448,1024]{3,2,1,0:T(8,128)(2,1)} %bitcast.66), custom_call_target="tpu_custom_call" | custom-call | flops 1879048192 | bytes 14680064 | tf_op jit(solution)/shard_map/branch/pallas_call | solution.py:101
  428.2 18.0 %all_to_all.45 = bf16[8,128,256]{2,1,0:T(8,128)(2,1)S(1)} all-to-all(bf16[8,128,256]{2,1,0:T(8,128)(2,1)} %branch.1), channel_id=1, replica_groups={{0,1,2,3,4,5,6,7},{8,9,10,11,12,13,14,15},{16,17,18,19,20,21,22,23},{24..., dimensions={0} | all-to-all | bytes 1048576 | tf_op jit(solution)/shard_map/all_to_all | solution.py:28
  (75 shorter events, 28.3 us)
Async XLA Ops:
  6.5 49.2 %copy-start.11 = (bf16[1024,448]{0,1:T(8,128)(2,1)S(1)}, bf16[1024,448]{0,1:T(8,128)(2,1)}, u32[]{:S(2)}) copy-start(bf16[1024,448]{0,1:T(8,128)(2,1)} %param.13) | copy-start | bytes 2752516
  6.5 361.0 %all-gather.7.cloned.1.call-start = ((), (), s32[]{:S(2)}) async-start(), calls=%async_computation.8 | async-start | bytes 8257536 | tf_op jit(solution)/shard_map/all_gather | solution.py:196
  6.5 44.9 %collective-permute-start = (bf16[448,1024]{1,0:T(8,128)(2,1)}, bf16[448,1024]{1,0:T(8,128)(2,1)S(1)}, u32[]{:S(2)}, u32[]{:S(2)}) collective-permute-start(bf16[448,1024]{1,0:T(8,128)(2,1)} %bitcast.95), channel_id=1, source_target_pairs={{0,0},{1,1},{2,2},{3,3},{4,4},{5,5},{6,6},{7,7},{8,64},{9,65},{10,... | collective-permute-start | bytes 2752520 | tf_op jit(solution)/shard_map/ppermute | solution.py:183
  51.4 0.9 copy-start.3
  55.7 51.7 %copy-start.12 = (bf16[1024,448]{0,1:T(8,128)(2,1)S(1)}, bf16[1024,448]{0,1:T(8,128)(2,1)}, u32[]{:S(2)}) copy-start(bf16[1024,448]{0,1:T(8,128)(2,1)} %param.14) | copy-start | bytes 2752516
  55.7 317.9 %all-gather.9.cloned.1.call-start = ((), (), s32[]{:S(2)}) async-start(), calls=%async_computation.9 | async-start | bytes 8257536 | tf_op jit(solution)/shard_map/all_gather | solution.py:196
  55.7 47.3 %collective-permute-start.1 = (bf16[448,1024]{1,0:T(8,128)(2,1)S(1)}, bf16[448,1024]{1,0:T(8,128)(2,1)S(1)}, u32[]{:S(2)}, u32[]{:S(2)}) collective-permute-start(bf16[448,1024]{1,0:T(8,128)(2,1)S(1)} %bitcast.96), channel_id=1, source_target_pairs={{0,0},{1,1},{2,2},{3,3},{4,4},{5,5},{6,6},{7,7},{8,64},{9,65},{10,... | collective-permute-start | bytes 2752520 | tf_op jit(solution)/shard_map/ppermute | solution.py:183
  103.0 0.9 copy-start.4
  107.3 46.3 %copy-start.8 = (s32[8,128]{1,0:T(8,128)S(1)}, s32[8,128]{1,0:T(8,128)}, u32[]{:S(2)}) copy-start(s32[8,128]{1,0:T(8,128)} %param.15) | copy-start | bytes 12292
  107.3 46.3 %copy-start.6 = (bf16[4,8192]{1,0:T(4,128)(2,1)S(1)}, bf16[4,8192]{1,0:T(4,128)(2,1)}, u32[]{:S(2)}) copy-start(bf16[4,8192]{1,0:T(4,128)(2,1)} %param.9) | copy-start | bytes 196612
  107.3 46.3 %copy-start.9 = (bf16[8,128]{1,0:T(8,128)(2,1)S(1)}, bf16[8,128]{1,0:T(8,128)(2,1)}, u32[]{:S(2)}) copy-start(bf16[8,128]{1,0:T(8,128)(2,1)} %param.16) | copy-start | bytes 6148
  107.3 46.4 %copy-start.7 = (bf16[4,8192]{1,0:T(4,128)(2,1)S(1)}, bf16[4,8192]{1,0:T(4,128)(2,1)}, u32[]{:S(2)}) copy-start(bf16[4,8192]{1,0:T(4,128)(2,1)} %param.10) | copy-start | bytes 196612
  107.3 272.2 %all-gather.11.cloned.1.call-start = ((), (), s32[]{:S(2)}) async-start(), calls=%async_computation.10 | async-start | bytes 8257536 | tf_op jit(solution)/shard_map/all_gather | solution.py:196
  107.4 42.0 %collective-permute-start.2 = (bf16[448,1024]{1,0:T(8,128)(2,1)S(1)}, bf16[448,1024]{1,0:T(8,128)(2,1)S(1)}, u32[]{:S(2)}, u32[]{:S(2)}) collective-permute-start(bf16[448,1024]{1,0:T(8,128)(2,1)S(1)} %bitcast.97), channel_id=1, source_target_pairs={{0,0},{1,1},{2,2},{3,3},{4,4},{5,5},{6,6},{7,7},{8,64},{9,65},{10,... | collective-permute-start | bytes 2752520 | tf_op jit(solution)/shard_map/ppermute | solution.py:183
  149.3 0.9 copy-start.5
  155.7 98.2 %all-to-all-start = ((bf16[32,344,128]{2,1,0:T(8,128)(2,1)}), bf16[32,344,128]{2,1,0:T(8,128)(2,1)S(1)}, u32[]{:S(2)}, u32[]{:S(2)}) async-start(bf16[32,344,128]{2,1,0:T(8,128)(2,1)} %bitcast.67), calls=%async_computation | async-start | bytes 5636096 | tf_op jit(solution)/shard_map/all_to_all | solution.py:28
  254.1 1.9 copy-start.10
  266.6 21.9 %copy-start = (f32[128,512]{1,0:T(8,128)S(1)}, f32[128,512]{1,0:T(8,128)}, u32[]{:S(2)}) copy-start(f32[128,512]{1,0:T(8,128)} %marks.1) | copy-start | bytes 786436
  349.2 17.5 %all-to-all-start.4 = ((bf16[8,128,256]{2,1,0:T(8,128)(2,1)}), bf16[8,128,256]{2,1,0:T(8,128)(2,1)S(1)}, u32[]{:S(2)}, u32[]{:S(2)}) async-start(bf16[8,128,256]{2,1,0:T(8,128)(2,1)} %broadcast_in_dim.62), calls=%async_computation.4 | async-start | bytes 1048576 | tf_op jit(solution)/shard_map/all_to_all | solution.py:28
  379.6 6.1 %copy-start.1 = (bf16[4,128,448]{2,1,0:T(8,128)(2,1)S(1)}, bf16[4,128,448]{2,1,0:T(8,128)(2,1)}, u32[]{:S(2)}) copy-start(bf16[4,128,448]{2,1,0:T(8,128)(2,1)} %wide.3) | copy-start | bytes 1376260
  379.6 6.1 %copy-start.2 = (bf16[4,128,448]{2,1,0:T(8,128)(2,1)S(1)}, bf16[4,128,448]{2,1,0:T(8,128)(2,1)}, u32[]{:S(2)}) copy-start(bf16[4,128,448]{2,1,0:T(8,128)(2,1)} %wide.4) | copy-start | bytes 1376260
Sparse Core Ops, SparseCore 0:
  55.8 89.1 all-gather.6
  146.9 64.1 all-gather.8
  212.9 47.9 all-gather.10

commit v2 on v1

--- a/solution.py
+++ b/solution.py
@@ -11,6 +11,20 @@
 
 Y_GROUPS = [[y * NZ + z for y in range(NY)] for z in range(NZ)]
 Z_GROUPS = [[y * NZ + z for z in range(NZ)] for y in range(NY)]
+X_GROUPS = [[x * CORES + c for x in range(NX)] for c in range(CORES)]
+YC_GROUPS = [
+    [(x * CORES + c) * NY * NZ + y * NZ + z for y in range(NY) for c in range(CORES)]
+    for x in range(NX)
+    for z in range(NZ)
+]
+
+
+def turns(dy, dz):
+    return [
+        (y * NZ + z, (y + dy) % NY * NZ + (z + dz) % NZ) for y in range(NY) for z in range(NZ)
+    ]
+
+
 SWAP_XY = [
     (
         (x * CORES + c) * NY * NZ + y * NZ + z,
@@ -22,10 +36,31 @@
     for z in range(NZ)
 ]
 NT = (((1,), (1,)), ((), ()))
-
-
-def exchange(blocks, groups=None):
-    return lax.all_to_all(blocks, "vocab", 0, 0, axis_index_groups=groups)
+TN = (((0,), (0,)), ((), ()))
+
+
+def exchange(blocks, groups=None, axis="vocab"):
+    return lax.all_to_all(blocks, axis, 0, 0, axis_index_groups=groups)
+
+
+def swap_xy(array):
+    return lax.ppermute(array, ("dp", "vocab"), SWAP_XY)
+
+
+def collect(block):
+    def turn(value, dy, dz):
+        return lax.ppermute(value, "vocab", turns(dy, dz))
+
+    ahead, behind = turn(block[None], 0, -1), turn(block[None], 0, 1)
+    near = jnp.concatenate([behind, block[None], ahead])
+    line = jnp.concatenate([turn(near, 0, 3), near, turn(near[:2], 0, -3)])
+    plane = jnp.concatenate([line, turn(line, -1, 0), turn(line, 1, 0), turn(line, 2, 0)])
+    place = lax.axis_index("vocab")
+    y, z = place // NZ, place % NZ
+    along = jnp.array([-4, -3, -2, -1, 0, 1, 2, 3], jnp.int32)
+    across = jnp.array([0, 1, -1, -2], jnp.int32)
+    source = ((y + across) % NY)[:, None] * NZ + ((z + along) % NZ)[None, :]
+    return plane, source.reshape(-1)
 
 
 def replicate(block, copies):
@@ -47,61 +82,69 @@
     return jnp.sum(blocks.astype(jnp.float32), axis=0)
 
 
-def wide_kernel(rows_ref, weight_ref, out_ref):
+def wide_kernel(rows_ref, weight_ref, *refs):
+    out_ref = refs[-1]
     half = weight_ref.shape[2]
     total = lax.dot_general(
-        rows_ref[:, :half], weight_ref[0], NT, preferred_element_type=jnp.float32
+        weight_ref[0], rows_ref[:, :half], NT, preferred_element_type=jnp.float32
     )
     total += lax.dot_general(
-        rows_ref[:, half:], weight_ref[1], NT, preferred_element_type=jnp.float32
-    )
-    out_ref[0] = total.astype(out_ref.dtype)
-
-
-def wide(rows, weight):
+        weight_ref[1], rows_ref[:, half:], NT, preferred_element_type=jnp.float32
+    )
+    out_ref[0, 0] = total.astype(out_ref.dtype)
+
+
+def wide(rows, weight, slot, buffer=None):
     count = rows.shape[0]
     blocks, hidden, half = weight.shape
     parts = blocks // CORES
+    in_specs = [
+        pl.BlockSpec(rows.shape, lambda i: (0, 0)),
+        pl.BlockSpec((CORES, hidden, half), lambda i: (i, 0, 0)),
+    ]
+    args = (rows, weight)
+    if buffer is not None:
+        in_specs.append(pl.BlockSpec(memory_space=pl.ANY))
+        args += (buffer,)
     return pl.pallas_call(
         wide_kernel,
         grid=(parts,),
-        in_specs=[
-            pl.BlockSpec(rows.shape, lambda i: (0, 0)),
-            pl.BlockSpec((CORES, hidden, half), lambda i: (i, 0, 0)),
-        ],
-        out_specs=pl.BlockSpec((1, count, hidden), lambda i: (i, 0, 0)),
-        out_shape=jax.ShapeDtypeStruct((parts, count, hidden), jnp.bfloat16),
+        in_specs=in_specs,
+        out_specs=pl.BlockSpec((1, 1, hidden, count), lambda i: (i, slot, 0, 0)),
+        out_shape=jax.ShapeDtypeStruct((parts, 3, hidden, count), jnp.bfloat16),
+        input_output_aliases={} if buffer is None else {2: 0},
         cost_estimate=pl.CostEstimate(
             flops=2 * count * blocks * hidden * half,
             bytes_accessed=2 * (weight.size + rows.size),
             transcendentals=0,
         ),
         name="wide",
-    )(rows, weight)
-
-
-def branch_kernel(gate_ref, up_ref, gate_weight_ref, up_weight_ref, out_ref):
+    )(*args)
+
+
+def branch_kernel(act_ref, gate_weight_ref, up_weight_ref, out_ref):
     total = None
-    for i in range(gate_ref.shape[0]):
-        for act, weight in ((gate_ref, gate_weight_ref), (up_ref, up_weight_ref)):
-            part = jnp.dot(act[i], weight[i, 0], preferred_element_type=jnp.float32)
+    for i in range(act_ref.shape[0]):
+        for k, weight in enumerate((gate_weight_ref, up_weight_ref)):
+            part = lax.dot_general(
+                act_ref[i, k], weight[i, 0], TN, preferred_element_type=jnp.float32
+            )
             total = part if total is None else total + part
     out_ref[0] = total.astype(out_ref.dtype)
 
 
-def branch_blocks(gate, up, gate_weight, up_weight):
-    parts, count, hidden = gate.shape
+def branch_blocks(acts, gate_weight, up_weight):
+    parts, _, hidden, count = acts.shape
     half = gate_weight.shape[2]
     share = CORES * half // NZ
     per = half // share
     gate_weight = gate_weight.reshape(parts, CORES, hidden, half)
     up_weight = up_weight.reshape(parts, CORES, hidden, half)
     weight_spec = pl.BlockSpec((parts, 1, hidden, share), lambda i: (0, i // per, 0, i % per))
-    act_spec = pl.BlockSpec(gate.shape, lambda i: (0, 0, 0))
     return pl.pallas_call(
         branch_kernel,
         grid=(NZ,),
-        in_specs=[act_spec, act_spec, weight_spec, weight_spec],
+        in_specs=[pl.BlockSpec(acts.shape, lambda i: (0, 0, 0, 0)), weight_spec, weight_spec],
         out_specs=pl.BlockSpec((1, count, share), lambda i: (i, 0, 0)),
         out_shape=jax.ShapeDtypeStruct((NZ, count, share), jnp.bfloat16),
         cost_estimate=pl.CostEstimate(
@@ -110,7 +153,7 @@
             transcendentals=0,
         ),
         name="branch",
-    )(gate, up, gate_weight, up_weight)
+    )(acts, gate_weight, up_weight)
 
 
 def head_kernel(grad_ref, weight_ref, out_ref):
@@ -175,25 +218,8 @@
     )(columns, probs)
 
 
-def land_kernel(moved_ref, out_ref):
-    out_ref[...] = moved_ref[...]
-
-
 def gather_weight(weight):
-    moved = lax.ppermute(weight.T, ("dp", "vocab"), SWAP_XY)
-    hidden, half = moved.shape
-    step = hidden // 4
-    spec = pl.BlockSpec((step, half), lambda i: (i, 0))
-    landed = pl.pallas_call(
-        land_kernel,
-        grid=(4,),
-        in_specs=[spec],
-        out_specs=spec,
-        out_shape=jax.ShapeDtypeStruct(moved.shape, moved.dtype),
-        cost_estimate=pl.CostEstimate(flops=0, bytes_accessed=4 * moved.size, transcendentals=0),
-        name="land",
-    )(moved)
-    return lax.all_gather(landed, "dp", axis=0)
+    return lax.all_gather(weight.T, ("dp", "vocab"), axis=0, axis_index_groups=YC_GROUPS)
 
 
 def layers(
@@ -219,35 +245,30 @@
     up_full = gather_weight(up_weight)
     down_full = gather_weight(down_weight)
 
-    tiles = width // 128
     quarter = width // NY
-    shared = jnp.concatenate(
-        [
-            as_tiles(head_input),
-            (tile_ids // RADIX).astype(jnp.bfloat16).reshape(-1, 128),
-            (tile_ids % RADIX).astype(jnp.bfloat16).reshape(-1, 128),
-            tile_probs.reshape(-1, 128),
-        ],
-        axis=0,
-    )
-    size = own_rows * tiles
+    head_tiles = as_tiles(head_input)
+    size = head_tiles.shape[0]
     packed = jnp.concatenate(
-        [replicate(shared, NY), as_tiles(body_input).reshape(NY, -1, 128)], axis=1
+        [replicate(head_tiles, NY), as_tiles(body_input).reshape(NY, -1, 128)], axis=1
     )
     packed = jnp.broadcast_to(packed[:, None], (NY, NZ) + packed.shape[1:])
     packed = packed.reshape((shards,) + packed.shape[2:])
     arrived = exchange(packed)
     head_rows = from_tiles(arrived[:, :size], own_rows)
-    body_rows = from_tiles(arrived[:, shared.shape[0] :], own_rows)
-    store = (
-        arrived[:, size : shared.shape[0]]
-        .reshape(shards, 3, slots, entries)
-        .transpose(0, 2, 1, 3)
-        .reshape(shards * slots, 3 * entries)
-    )
-    chosen_slot = (
-        tile_slot[:, None] == lax.broadcasted_iota(jnp.int32, (count, shards * slots), 1)
-    ).astype(jnp.bfloat16)
+    body_rows = swap_xy(from_tiles(arrived[:, size:], own_rows))
+
+    tile = jnp.concatenate(
+        [
+            (tile_ids // RADIX).astype(jnp.bfloat16),
+            (tile_ids % RADIX).astype(jnp.bfloat16),
+            tile_probs,
+        ],
+        axis=1,
+    )
+    store, source = collect(tile)
+    store = store.reshape(shards * slots, 3 * entries)
+    store_slot = (source[:, None] * slots + jnp.arange(slots, dtype=jnp.int32)).reshape(1, -1)
+    chosen_slot = (tile_slot[:, None] == store_slot).astype(jnp.bfloat16)
     found = jnp.dot(chosen_slot, store, preferred_element_type=jnp.float32)
     row_ids = (found[:, :entries] * RADIX + found[:, entries : 2 * entries]).astype(jnp.int32)
     row_probs = found[:, 2 * entries :]
@@ -265,7 +286,8 @@
         jnp.where(picked, 0.0, jnp.exp(rest - local_rest_max)), axis=1, keepdims=True
     )
     stats = jnp.concatenate([local_max, local_rest_max, local_top, local_rest], axis=1).T
-    maxima, rest_maxima, tops, rests = jnp.split(exchange(replicate(stats, shards)), 4, axis=1)
+    every = exchange(replicate(stats, shards))
+    maxima, rest_maxima, tops, rests = jnp.split(every, 4, axis=1)
     row_max = jnp.max(maxima, axis=0)
     rest_max = jnp.max(rest_maxima, axis=0)
     top_sum = jnp.sum(tops * jnp.exp(maxima - row_max), axis=0)
@@ -284,25 +306,26 @@
         )
     ).astype(jnp.bfloat16)
 
-    gate_part = wide(body_rows, gate_full)
-    up_part = wide(body_rows, up_full)
+    parts = wide(body_rows, gate_full, 0)
+    parts = wide(body_rows, up_full, 1, parts)
 
     partial = head_blocks(logit_grad, head_weight).reshape(NY, NZ, count, share)
-    over_y = add_blocks(exchange(partial, Y_GROUPS)).astype(jnp.bfloat16)
+    arrived = exchange(partial, Y_GROUPS)
+    over_y = add_blocks(arrived).astype(jnp.bfloat16)
     head_own = add_blocks(exchange(over_y, Z_GROUPS)).astype(jnp.bfloat16)
+    head_own = swap_xy(head_own)
     head_grad = (
         exchange(replicate(head_own, NZ), Z_GROUPS).transpose(1, 0, 2).reshape(count, quarter)
     )
 
-    parts = jnp.stack([gate_part, up_part, wide(head_grad, down_full)], axis=1)
-    gate_act, up_act, down_grad = add_blocks(exchange(parts, Y_GROUPS))
+    parts = wide(head_grad, down_full, 2, parts)
+    gate_act, up_act, down_grad = add_blocks(exchange(parts, X_GROUPS, "dp"))
     sigma = 1.0 / (1.0 + jnp.exp(-gate_act))
     gate_grad = (down_grad * up_act * sigma * (1.0 + gate_act * (1.0 - sigma))).astype(jnp.bfloat16)
     up_grad = (down_grad * gate_act * sigma).astype(jnp.bfloat16)
-    both = exchange(replicate(jnp.stack([gate_grad, up_grad]), NY), Y_GROUPS)
-    pieces = branch_blocks(both[:, 0], both[:, 1], gate_full, up_full)
-    summed = add_blocks(exchange(pieces, Z_GROUPS))
-    return (head_own.astype(jnp.float32) + summed).astype(jnp.bfloat16)
+    both = exchange(replicate(jnp.stack([gate_grad, up_grad]), NX), X_GROUPS, "dp")
+    summed = add_blocks(exchange(branch_blocks(both, gate_full, up_full), Z_GROUPS))
+    return swap_xy((head_own.astype(jnp.float32) + summed).astype(jnp.bfloat16))
 
 
 def solution(mesh):

time: 455 us -> 348 us (0.76)
  waiting for transfers between devices: 202 us -> 82.7 us
  blocking collectives: 108 us -> 141 us
  Pallas kernels: 55 us -> 44.8 us
  local copies, waits for them, and re-layouts: 13.5 us -> 7.69 us
    all_to_all x2, waiting for transfers between devices: 79.9 us -> 10.2 us  [exchange(): return lax.all_to_all(blocks, axis, 0, 0, axis_index_groups=groups)]
    ppermute x3 -> x10, waiting for transfers between devices: 122 us -> 70.4 us  [the longest x7 60.7 us: turn(): return lax.ppermute(value, 'vocab', turns(dy, dz))]
    all_to_all x6, blocking collectives: 108 us -> 141 us  [exchange(): return lax.all_to_all(blocks, axis, 0, 0, axis_index_groups=groups)]
    all_to_all x2, starting transfers between devices: 34 us -> 15.8 us  [exchange(): return lax.all_to_all(blocks, axis, 0, 0, axis_index_groups=groups)]
    ppermute x3 -> x10, starting transfers between devices: 12.5 us -> 26.5 us  [the longest x7 14.1 us: turn(): return lax.ppermute(value, 'vocab', turns(dy, dz))]
    pallas_call x7 -> x4, Pallas kernels: 37.9 us -> 27.6 us  [the longest x3 17.6 us: wide(): pl.pallas_call(wide_kernel, grid=(parts,), in_specs=in_specs, out_specs=p...]
  transfers between devices with their start and end apart: 8 -> 15, of which waited for: 5 -> 8; matrix products, arithmetic and copies ran while one was open for 5% -> 5% of each run, Pallas kernels for 8% -> 8%
where the time goes in v2:
time: 348 us; the launch traced here: 345 us
  blocking collectives  141 us (41%)
  waiting for transfers between devices  82.7 us (24%)
  Pallas kernels  44.8 us (13%)
  starting transfers between devices  42.3 us (12%)
  between operations  13.4 us (4%)
  local copies, waits for them, and re-layouts  7.69 us (2%)
  matrix products  7.03 us (2%)
  other arithmetic  6.14 us (2%)
    all_to_all x6, blocking collectives, exchange(): return lax.all_to_all(blocks, axis, 0, 0, axis_index_groups=groups)  141 us
    ppermute x7, waiting for transfers between devices, turn(): return lax.ppermute(value, 'vocab', turns(dy, dz))  60.7 us
    pallas_call x3, Pallas kernels, wide(): pl.pallas_call(wide_kernel, grid=(parts,), in_specs=in_specs, out_specs=p...  17.6 us
    all_to_all x2, starting transfers between devices, exchange(): return lax.all_to_all(blocks, axis, 0, 0, axis_index_groups=groups)  15.8 us
    ppermute x7, starting transfers between devices, turn(): return lax.ppermute(value, 'vocab', turns(dy, dz))  14.1 us
    ppermute x3, starting transfers between devices, swap_xy(): return lax.ppermute(array, ('dp', 'vocab'), SWAP_XY)  12.3 us
    all_to_all x2, waiting for transfers between devices, exchange(): return lax.all_to_all(blocks, axis, 0, 0, axis_index_groups=groups)  10.2 us
    pallas_call x1, Pallas kernels, branch_blocks(): pl.pallas_call(branch_kernel, grid=(NZ,), in_specs=[pl.BlockSpec(acts.sha...  10 us
  transfers between devices with their start and end apart: 15, of which 8 were waited for; matrix products, arithmetic and copies ran while one was open for 5% of the time, Pallas kernels for 8%

profile of v2, /device:TPU:2, one launch (start us, length us, event | category | flops | bytes accessed | tf_op | source)
XLA Modules:
  0.0 344.9 jit_solution(1863617942453319250)
XLA Ops:
  11.0 11.6 %all-to-all-start = ((bf16[32,320,128]{2,1,0:T(8,128)(2,1)}), bf16[32,320,128]{2,1,0:T(8,128)(2,1)S(1)}, u32[]{:S(2)}, u32[]{:S(2)}) async-start(bf16[32,320,128]{2,1,0:T(8,128)(2,1)} %bitcast.64), calls=%async_computation | async-start | bytes 5242880 | tf_op jit(solution)/shard_map/all_to_all | solution.py:43
  26.2 55.6 %collective-permute-done = bf16[1,8,384]{2,1,0:T(8,128)(2,1)S(1)} collective-permute-done((bf16[1,8,384]{2,1,0:T(8,128)(2,1)S(1)}, bf16[1,8,384]{2,1,0:T(8,128)(2,1)S(1)}, u32[]{:S(2)}, u32[]{:S(2)}) %collective-permute-start) | collective-permute-done | bytes 6176 | tf_op jit(solution)/shard_map/ppermute | solution.py:52
  83.5 3.4 collective-permute-start.3
  89.0 2.9 collective-permute-start.4
  94.9 3.1 collective-permute-done.5
  99.5 9.1 %marks.1 = f32[128,512]{1,0:T(8,128)} custom-call(s32[128,128]{1,0:T(8,128)} %fusion.11.columns_ref, f32[128,128]{1,0:T(8,128)} %get-tuple-element.15.probs_ref), custom_call_target="tpu_custom_call" | custom-call | flops 16777216 | bytes 262144 | tf_op jit(solution)/shard_map/marks/pallas_call | solution.py:208
  109.8 6.8 %fusion.21 = (f32[128]{0:T(128)S(1)}, f32[128]{0:T(128)S(1)}, pred[128,512]{1,0:T(8,128)(4,1)S(1)}, f32[128,512]{1,0:T(8,128)S(1)}) fusion(f32[128,512]{1,0:T(8,128)S(1)} %copy-done, bf16[512,8192]{1,0:T(8,128)(2,1)} %weight_ref.1, bf16[16,8,64,128]{3,2,1,0:T(8,128)(2,1)S(1)} %bitcast.66), kind=kOutput, calls=%fused_computation.75 | convolution fusion | flops 1074003712 | bytes 11076608 | tf_op jit(solution)/shard_map/rd,vd->rv/dot_general | solution.py:280
  116.9 18.5 %all_to_all.40 = f32[32,4,128]{2,1,0:T(4,128)S(1)} all-to-all(f32[32,4,128]{2,1,0:T(4,128)S(1)} %broadcast_in_dim.72), channel_id=1, replica_groups=mesh['dp'=8,'vocab'=32] {'vocab'}, dimensions={0} | all-to-all | bytes 131072 | tf_op jit(solution)/shard_map/all_to_all | solution.py:43
  136.5 8.0 %head.1 = bf16[32,128,256]{2,1,0:T(8,128)(2,1)} custom-call(bf16[128,512]{1,0:T(8,128)(2,1)} %multiply_convert_fusion.grad_ref, bf16[512,8192]{1,0:T(8,128)(2,1)} %weight_ref.1), custom_call_target="tpu_custom_call" | custom-call | flops 1073741824 | bytes 8388608 | tf_op jit(solution)/shard_map/head/pallas_call | solution.py:175
  144.5 48.2 %all_to_all.41 = bf16[4,8,128,256]{3,2,1,0:T(8,128)(2,1)} all-to-all(bf16[4,8,128,256]{3,2,1,0:T(8,128)(2,1)} %bitcast.67), channel_id=1, replica_groups={{0,8,16,24},{1,9,17,25},{2,10,18,26},{3,11,19,27},{4,12,20,28},{5,13,21..., dimensions={0} | all-to-all | bytes 4194304 | tf_op jit(solution)/shard_map/all_to_all | solution.py:43
  192.7 2.9 reduce_sum.92
  195.6 19.0 %all_to_all.42 = bf16[8,128,256]{2,1,0:T(8,128)(2,1)S(1)} all-to-all(bf16[8,128,256]{2,1,0:T(8,128)(2,1)} %reduce_sum.92), channel_id=1, replica_groups={{0,1,2,3,4,5,6,7},{8,9,10,11,12,13,14,15},{16,17,18,19,20,21,22,23},{24..., dimensions={0} | all-to-all | bytes 1048576 | tf_op jit(solution)/shard_map/all_to_all | solution.py:43
  216.7 5.2 %collective-permute-done.7 = bf16[128,256]{1,0:T(8,128)(2,1)S(1)} collective-permute-done((bf16[128,256]{1,0:T(8,128)(2,1)S(1)}, bf16[128,256]{1,0:T(8,128)(2,1)S(1)}, u32[]{:S(2)}, u32[]{:S(2)}) %collective-permute-start.7) | collective-permute-done | bytes 65568 | tf_op jit(solution)/shard_map/ppermute | solution.py:47
  222.7 4.2 %all-to-all-start.4 = ((bf16[8,128,256]{2,1,0:T(8,128)(2,1)}), bf16[8,128,256]{2,1,0:T(8,128)(2,1)S(1)}, u32[]{:S(2)}, u32[]{:S(2)}) async-start(bf16[8,128,256]{2,1,0:T(8,128)(2,1)} %broadcast_in_dim.73), calls=%async_computation.4 | async-start | bytes 1048576 | tf_op jit(solution)/shard_map/all_to_all | solution.py:43
  230.0 10.2 %all-to-all-done.4 = bf16[8,128,256]{2,1,0:T(8,128)(2,1)S(1)} async-done(((bf16[8,128,256]{2,1,0:T(8,128)(2,1)}), bf16[8,128,256]{2,1,0:T(8,128)(2,1)S(1)}, u32[]{:S(2)}, u32[]{:S(2)}) %all-to-all-start.4) | async-done | bytes 524320 | tf_op jit(solution)/shard_map/all_to_all | solution.py:43
  243.4 5.9 %wide.3.refs_0_ = bf16[4,3,448,128]{3,2,1,0:T(8,128)(2,1)} custom-call(bf16[128,2048]{1,0:T(8,128)(2,1)} %copy-done.1, bf16[8,448,1024]{2,1,0:T(8,128)(2,1)} %bitcast.60), custom_call_target="tpu_custom_call" | custom-call | flops 939524096 | bytes 7864320 | tf_op jit(solution)/shard_map/wide/pallas_call | solution.py:109
  249.2 5.9 %wide.4.refs_0_ = bf16[4,3,448,128]{3,2,1,0:T(8,128)(2,1)} custom-call(bf16[128,2048]{1,0:T(8,128)(2,1)} %copy-done.1, bf16[8,448,1024]{2,1,0:T(8,128)(2,1)} %bitcast.62, bf16[4,3,448,128]{3,2,1,0:T(8,128)(2,1)} %wide.3.refs_0_), custom_call_target="tpu_custom_call", output_to_operand_aliasing={{}: (2, {})} | custom-call | flops 939524096 | bytes 7864320 | tf_op jit(solution)/shard_map/wide/pallas_call | solution.py:109
  255.1 5.9 %wide.5 = bf16[4,3,448,128]{3,2,1,0:T(8,128)(2,1)} custom-call(bf16[128,2048]{1,0:T(8,128)(2,1)} %bitcast.72, bf16[8,448,1024]{2,1,0:T(8,128)(2,1)} %bitcast.68, bf16[4,3,448,128]{3,2,1,0:T(8,128)(2,1)} %wide.4.refs_0_), custom_call_target="tpu_custom_call", output_to_operand_aliasing={{}: (2, {})} | custom-call | flops 939524096 | bytes 7864320 | tf_op jit(solution)/shard_map/wide/pallas_call | solution.py:109
  261.0 21.4 %all_to_all.43 = bf16[4,3,448,128]{3,2,1,0:T(8,128)(2,1)S(1)} all-to-all(bf16[4,3,448,128]{3,2,1,0:T(8,128)(2,1)} %wide.5), channel_id=1, replica_groups={{0,64,128,192},{32,96,160,224},{1,65,129,193},{33,97,161,225},{2,66,130..., dimensions={0} | all-to-all | bytes 2752512 | tf_op jit(solution)/shard_map/all_to_all | solution.py:43
  282.8 13.3 %all_to_all.44.act_ref = bf16[4,2,448,128]{3,2,1,0:T(8,128)(2,1)} all-to-all(bf16[4,2,448,128]{3,2,1,0:T(8,128)(2,1)S(1)} %broadcast_in_dim.74), channel_id=1, replica_groups={{0,64,128,192},{32,96,160,224},{1,65,129,193},{33,97,161,225},{2,66,130..., dimensions={0} | all-to-all | bytes 1835008 | tf_op jit(solution)/shard_map/all_to_all | solution.py:43
  296.2 10.0 %branch.1 = bf16[8,128,256]{2,1,0:T(8,128)(2,1)} custom-call(bf16[4,2,448,128]{3,2,1,0:T(8,128)(2,1)} %all_to_all.44.act_ref, bf16[4,2,448,1024]{3,2,1,0:T(8,128)(2,1)} %bitcast.61, bf16[4,2,448,1024]{3,2,1,0:T(8,128)(2,1)} %bitcast.63), custom_call_target="tpu_custom_call" | custom-call | flops 1879048192 | bytes 14680064 | tf_op jit(solution)/shard_map/branch/pallas_call | solution.py:144
  306.2 20.5 %all_to_all.45 = bf16[8,128,256]{2,1,0:T(8,128)(2,1)S(1)} all-to-all(bf16[8,128,256]{2,1,0:T(8,128)(2,1)} %branch.1), channel_id=1, replica_groups={{0,1,2,3,4,5,6,7},{8,9,10,11,12,13,14,15},{16,17,18,19,20,21,22,23},{24..., dimensions={0} | all-to-all | bytes 1048576 | tf_op jit(solution)/shard_map/all_to_all | solution.py:43
  326.8 8.0 %collective-permute-start.9 = (bf16[128,256]{1,0:T(8,128)(2,1)S(1)}, bf16[128,256]{1,0:T(8,128)(2,1)S(1)}, u32[]{:S(2)}, u32[]{:S(2)}) collective-permute-start(bf16[128,256]{1,0:T(8,128)(2,1)S(1)} %add_convert_fusion), channel_id=1, source_target_pairs={{0,0},{1,1},{2,2},{3,3},{4,4},{5,5},{6,6},{7,7},{8,64},{9,65},{10,... | collective-permute-start | bytes 196616 | tf_op jit(solution)/shard_map/ppermute | solution.py:47
  334.8 2.9 collective-permute-done.9
  (90 shorter events, 29.1 us)
Async XLA Ops:
  6.5 2.2 copy-start.2
  6.5 2.3 copy-start.3
  6.5 236.0 %all-gather.11.cloned.1.call-start = ((), (), s32[]{:S(2)}) async-start(), calls=%async_computation.10 | async-start | bytes 8257536 | tf_op jit(solution)/shard_map/all_gather | solution.py:222
  7.3 242.0 %all-gather.9.cloned.1.call-start = ((), (), s32[]{:S(2)}) async-start(), calls=%async_computation.9 | async-start | bytes 8257536 | tf_op jit(solution)/shard_map/all_gather | solution.py:222
  8.0 247.1 %all-gather.7.cloned.1.call-start = ((), (), s32[]{:S(2)}) async-start(), calls=%async_computation.8 | async-start | bytes 8257536 | tf_op jit(solution)/shard_map/all_gather | solution.py:222
  10.9 11.7 %copy-start.5 = (s32[8,128]{1,0:T(8,128)S(1)}, s32[8,128]{1,0:T(8,128)}, u32[]{:S(2)}) copy-start(s32[8,128]{1,0:T(8,128)} %param.17) | copy-start | bytes 12292
  10.9 11.7 %copy-start.4 = (bf16[8,128]{1,0:T(8,128)(2,1)S(1)}, bf16[8,128]{1,0:T(8,128)(2,1)}, u32[]{:S(2)}) copy-start(bf16[8,128]{1,0:T(8,128)(2,1)} %param.18) | copy-start | bytes 6148
  10.9 15.0 %copy-start.8 = (s32[8]{0:T(128)S(1)}, s32[8]{0:T(128)}, u32[]{:S(2)}) copy-start(s32[8]{0:T(128)} %constant.100.clone) | copy-start | bytes 100
  10.9 15.0 %copy-start.7 = (s32[4]{0:T(128)S(1)}, s32[4]{0:T(128)}, u32[]{:S(2)}) copy-start(s32[4]{0:T(128)} %constant.101.clone) | copy-start | bytes 52
  10.9 87.1 %copy-start.6 = (s32[128]{0:T(128)S(1)}, s32[128]{0:T(128)}, u32[]{:S(2)}) copy-start(s32[128]{0:T(128)} %param.19) | copy-start | bytes 1540
  11.0 97.7 %all-to-all-start = ((bf16[32,320,128]{2,1,0:T(8,128)(2,1)}), bf16[32,320,128]{2,1,0:T(8,128)(2,1)S(1)}, u32[]{:S(2)}, u32[]{:S(2)}) async-start(bf16[32,320,128]{2,1,0:T(8,128)(2,1)} %bitcast.64), calls=%async_computation | async-start | bytes 5242880 | tf_op jit(solution)/shard_map/all_to_all | solution.py:43
  22.6 59.1 %collective-permute-start = (bf16[1,8,384]{2,1,0:T(8,128)(2,1)S(1)}, bf16[1,8,384]{2,1,0:T(8,128)(2,1)S(1)}, u32[]{:S(2)}, u32[]{:S(2)}) collective-permute-start(bf16[1,8,384]{2,1,0:T(8,128)(2,1)S(1)} %maximum_bitcast_fusion), channel_id=1, source_target_pairs={{0,1},{1,2},{2,3},{3,4},{4,5},{5,6},{6,7},{7,0},{8,9},{9,10},{10,1... | collective-permute-start | bytes 18440 | tf_op jit(solution)/shard_map/ppermute | solution.py:52
  24.5 57.3 %collective-permute-start.1 = (bf16[1,8,384]{2,1,0:T(8,128)(2,1)S(1)}, bf16[1,8,384]{2,1,0:T(8,128)(2,1)S(1)}, u32[]{:S(2)}, u32[]{:S(2)}) collective-permute-start(bf16[1,8,384]{2,1,0:T(8,128)(2,1)S(1)} %maximum_bitcast_fusion), channel_id=1, source_target_pairs={{0,7},{1,0},{2,1},{3,2},{4,3},{5,4},{6,5},{7,6},{8,15},{9,8},{10,9... | collective-permute-start | bytes 18440 | tf_op jit(solution)/shard_map/ppermute | solution.py:52
  81.8 6.8 %collective-permute-start.2 = (bf16[3,8,384]{2,1,0:T(8,128)(2,1)S(1)}, bf16[3,8,384]{2,1,0:T(8,128)(2,1)S(1)}, u32[]{:S(2)}, u32[]{:S(2)}) collective-permute-start(bf16[3,8,384]{2,1,0:T(8,128)(2,1)S(1)} %pad_maximum_fusion.2), channel_id=1, source_target_pairs={{0,3},{1,4},{2,5},{3,6},{4,7},{5,0},{6,1},{7,2},{8,11},{9,12},{10,... | collective-permute-start | bytes 55304 | tf_op jit(solution)/shard_map/ppermute | solution.py:52
  83.5 5.5 %collective-permute-start.3 = (bf16[2,8,384]{2,1,0:T(8,128)(2,1)S(1)}, bf16[2,8,384]{2,1,0:T(8,128)(2,1)S(1)}, u32[]{:S(2)}, u32[]{:S(2)}) collective-permute-start(bf16[2,8,384]{2,1,0:T(8,128)(2,1)S(1)} %pad_maximum_fusion.3), channel_id=1, source_target_pairs={{0,5},{1,6},{2,7},{3,0},{4,1},{5,2},{6,3},{7,4},{8,13},{9,14},{10,... | collective-permute-start | bytes 36872 | tf_op jit(solution)/shard_map/ppermute | solution.py:52
  89.0 5.9 %collective-permute-start.4 = (bf16[8,8,384]{2,1,0:T(8,128)(2,1)S(1)}, bf16[8,8,384]{2,1,0:T(8,128)(2,1)S(1)}, u32[]{:S(2)}, u32[]{:S(2)}) collective-permute-start(bf16[8,8,384]{2,1,0:T(8,128)(2,1)S(1)} %get-tuple-element.22), channel_id=1, source_target_pairs={{0,24},{1,25},{2,26},{3,27},{4,28},{5,29},{6,30},{7,31},{8,0},{9,1... | collective-permute-start | bytes 147464 | tf_op jit(solution)/shard_map/ppermute | solution.py:52
  92.1 5.9 %collective-permute-start.5 = (bf16[8,8,384]{2,1,0:T(8,128)(2,1)S(1)}, bf16[8,8,384]{2,1,0:T(8,128)(2,1)S(1)}, u32[]{:S(2)}, u32[]{:S(2)}) collective-permute-start(bf16[8,8,384]{2,1,0:T(8,128)(2,1)S(1)} %get-tuple-element.22), channel_id=1, source_target_pairs={{0,8},{1,9},{2,10},{3,11},{4,12},{5,13},{6,14},{7,15},{8,16},{9,17... | collective-permute-start | bytes 147464 | tf_op jit(solution)/shard_map/ppermute | solution.py:52
  92.2 5.8 %collective-permute-start.6 = (bf16[8,8,384]{2,1,0:T(8,128)(2,1)S(1)}, bf16[8,8,384]{2,1,0:T(8,128)(2,1)S(1)}, u32[]{:S(2)}, u32[]{:S(2)}) collective-permute-start(bf16[8,8,384]{2,1,0:T(8,128)(2,1)S(1)} %get-tuple-element.22), channel_id=1, source_target_pairs={{0,16},{1,17},{2,18},{3,19},{4,20},{5,21},{6,22},{7,23},{8,24},{9,... | collective-permute-start | bytes 147464 | tf_op jit(solution)/shard_map/ppermute | solution.py:52
  108.8 1.0 copy-start
  214.6 7.2 %collective-permute-start.7 = (bf16[128,256]{1,0:T(8,128)(2,1)S(1)}, bf16[128,256]{1,0:T(8,128)(2,1)S(1)}, u32[]{:S(2)}, u32[]{:S(2)}) collective-permute-start(bf16[128,256]{1,0:T(8,128)(2,1)S(1)} %reduce_sum.93), channel_id=1, source_target_pairs={{0,0},{1,1},{2,2},{3,3},{4,4},{5,5},{6,6},{7,7},{8,64},{9,65},{10,... | collective-permute-start | bytes 196616 | tf_op jit(solution)/shard_map/ppermute | solution.py:47
  222.7 17.5 %all-to-all-start.4 = ((bf16[8,128,256]{2,1,0:T(8,128)(2,1)}), bf16[8,128,256]{2,1,0:T(8,128)(2,1)S(1)}, u32[]{:S(2)}, u32[]{:S(2)}) async-start(bf16[8,128,256]{2,1,0:T(8,128)(2,1)} %broadcast_in_dim.73), calls=%async_computation.4 | async-start | bytes 1048576 | tf_op jit(solution)/shard_map/all_to_all | solution.py:43
  227.7 14.8 %collective-permute-start.8 = (bf16[128,2048]{1,0:T(8,128)(2,1)S(1)}, bf16[128,2048]{1,0:T(8,128)(2,1)S(1)}, u32[]{:S(2)}, u32[]{:S(2)}) collective-permute-start(bf16[128,2048]{1,0:T(8,128)(2,1)S(1)} %bitcast.76), channel_id=1, source_target_pairs={{0,0},{1,1},{2,2},{3,3},{4,4},{5,5},{6,6},{7,7},{8,64},{9,65},{10,... | collective-permute-start | bytes 1572872 | tf_op jit(solution)/shard_map/ppermute | solution.py:47
  242.6 0.8 copy-start.1
  326.8 11.0 %collective-permute-start.9 = (bf16[128,256]{1,0:T(8,128)(2,1)S(1)}, bf16[128,256]{1,0:T(8,128)(2,1)S(1)}, u32[]{:S(2)}, u32[]{:S(2)}) collective-permute-start(bf16[128,256]{1,0:T(8,128)(2,1)S(1)} %add_convert_fusion), channel_id=1, source_target_pairs={{0,0},{1,1},{2,2},{3,3},{4,4},{5,5},{6,6},{7,7},{8,64},{9,65},{10,... | collective-permute-start | bytes 196616 | tf_op jit(solution)/shard_map/ppermute | solution.py:47
Sparse Core Ops, SparseCore 0:
  9.2 76.1 all-gather.10
  87.2 47.6 all-gather.8
  136.8 64.3 all-gather.6

commit v3 on v2

--- a/solution.py
+++ b/solution.py
@@ -2,6 +2,7 @@
 import jax.numpy as jnp
 from jax import lax
 from jax.experimental import pallas as pl
+from jax.experimental.pallas import tpu as pltpu
 from jax.sharding import PartitionSpec as P
 
 
@@ -18,13 +19,10 @@
     for z in range(NZ)
 ]
 
-
-def turns(dy, dz):
-    return [
-        (y * NZ + z, (y + dy) % NY * NZ + (z + dz) % NZ) for y in range(NY) for z in range(NZ)
-    ]
-
-
+X_TURNS = {
+    step: [(x * CORES + c, (x + step) % NX * CORES + c) for x in range(NX) for c in range(CORES)]
+    for step in range(1, NX)
+}
 SWAP_XY = [
     (
         (x * CORES + c) * NY * NZ + y * NZ + z,
@@ -47,22 +45,6 @@
     return lax.ppermute(array, ("dp", "vocab"), SWAP_XY)
 
 
-def collect(block):
-    def turn(value, dy, dz):
-        return lax.ppermute(value, "vocab", turns(dy, dz))
-
-    ahead, behind = turn(block[None], 0, -1), turn(block[None], 0, 1)
-    near = jnp.concatenate([behind, block[None], ahead])
-    line = jnp.concatenate([turn(near, 0, 3), near, turn(near[:2], 0, -3)])
-    plane = jnp.concatenate([line, turn(line, -1, 0), turn(line, 1, 0), turn(line, 2, 0)])
-    place = lax.axis_index("vocab")
-    y, z = place // NZ, place % NZ
-    along = jnp.array([-4, -3, -2, -1, 0, 1, 2, 3], jnp.int32)
-    across = jnp.array([0, 1, -1, -2], jnp.int32)
-    source = ((y + across) % NY)[:, None] * NZ + ((z + along) % NZ)[None, :]
-    return plane, source.reshape(-1)
-
-
 def replicate(block, copies):
     return jnp.broadcast_to(block[None], (copies,) + block.shape)
 
@@ -94,7 +76,7 @@
     out_ref[0, 0] = total.astype(out_ref.dtype)
 
 
-def wide(rows, weight, slot, buffer=None):
+def wide(rows, weight, slot, entries, buffer=None):
     count = rows.shape[0]
     blocks, hidden, half = weight.shape
     parts = blocks // CORES
@@ -111,7 +93,7 @@
         grid=(parts,),
         in_specs=in_specs,
         out_specs=pl.BlockSpec((1, 1, hidden, count), lambda i: (i, slot, 0, 0)),
-        out_shape=jax.ShapeDtypeStruct((parts, 3, hidden, count), jnp.bfloat16),
+        out_shape=jax.ShapeDtypeStruct((parts, entries, hidden, count), jnp.bfloat16),
         input_output_aliases={} if buffer is None else {2: 0},
         cost_estimate=pl.CostEstimate(
             flops=2 * count * blocks * hidden * half,
@@ -190,32 +172,71 @@
     )(grad, weight)
 
 
-def marks_kernel(columns_ref, probs_ref, out_ref):
-    _, entries = columns_ref.shape
-    lanes = lax.broadcasted_iota(jnp.int32, out_ref.shape, 1)
+def score_kernel(
+    blocks_ref, low_ref, high_ref, columns_ref, probs_ref, logits_ref, marks_ref, low_sum, high_sum
+):
+    step = pl.program_id(0)
+    shards, size, lanes = blocks_ref.shape
+    both = 2 * logits_ref.shape[1]
+    rows = jnp.concatenate(
+        [
+            blocks_ref[:, i * both : (i + 1) * both].reshape(shards * both, lanes)
+            for i in range(size // both)
+        ],
+        axis=1,
+    )
+    for weight_ref, total in ((low_ref, low_sum), (high_ref, high_sum)):
+        part = lax.dot_general(rows, weight_ref[...], NT, preferred_element_type=jnp.float32)
+        total[...] = jnp.where(step == 0, 0.0, total[...]) + part
+    entries = columns_ref.shape[1]
+    places = lax.broadcasted_iota(jnp.int32, marks_ref.shape, 1)
     columns = columns_ref[...]
     probs = probs_ref[...]
-    marks = jnp.full(out_ref.shape, -1.0, jnp.float32)
+    marks = jnp.full(marks_ref.shape, -1.0, jnp.float32)
     for k in range(entries):
-        marks = jnp.where(lanes == columns[:, k : k + 1], probs[:, k : k + 1], marks)
-    out_ref[...] = marks
-
-
-def make_marks(columns, probs, vocab):
+        marks = jnp.where(places == columns[:, k : k + 1], probs[:, k : k + 1], marks)
+    marks_ref[...] = marks
+
+    @pl.when(step == pl.num_programs(0) - 1)
+    def _():
+        low = low_sum[...].reshape(shards, both, -1)
+        high = high_sum[...].reshape(shards, both, -1)
+        logits_ref[...] = low[:, : both // 2] + high[:, both // 2 :]
+
+
+def score(blocks, weight, columns, probs):
+    shards = blocks.shape[0]
     count, entries = columns.shape
-    step = 16
-    spec = pl.BlockSpec((step, entries), lambda i: (i, 0))
+    vocab, width = weight.shape
+    own_rows = count // shards
+    steps = 8
+    chunk = width // 2 // steps
+    size = chunk // 128 * 2 * own_rows
+    band = pl.BlockSpec((count // steps, entries), lambda i: (i, 0))
     return pl.pallas_call(
-        marks_kernel,
-        grid=(count // step,),
-        in_specs=[spec, spec],
-        out_specs=pl.BlockSpec((step, vocab), lambda i: (i, 0)),
-        out_shape=jax.ShapeDtypeStruct((count, vocab), jnp.float32),
+        score_kernel,
+        grid=(steps,),
+        in_specs=[
+            pl.BlockSpec((shards, size, 128), lambda i: (0, i, 0)),
+            pl.BlockSpec((vocab, chunk), lambda i: (0, i)),
+            pl.BlockSpec((vocab, chunk), lambda i: (0, i + steps)),
+            band,
+            band,
+        ],
+        out_specs=[
+            pl.BlockSpec((shards, own_rows, vocab), lambda i: (0, 0, 0)),
+            pl.BlockSpec((count // steps, vocab), lambda i: (i, 0)),
+        ],
+        out_shape=[
+            jax.ShapeDtypeStruct((shards, own_rows, vocab), jnp.float32),
+            jax.ShapeDtypeStruct((count, vocab), jnp.float32),
+        ],
+        scratch_shapes=[pltpu.VMEM((2 * count, vocab), jnp.float32)] * 2,
         cost_estimate=pl.CostEstimate(
-            flops=2 * count * entries * vocab, bytes_accessed=4 * count * vocab, transcendentals=0
-        ),
-        name="marks",
-    )(columns, probs)
+            flops=2 * count * weight.size, bytes_accessed=2 * weight.size, transcendentals=0
+        ),
+        name="score",
+    )(blocks, weight, weight, columns, probs)
 
 
 def gather_weight(weight):
@@ -246,38 +267,41 @@
     down_full = gather_weight(down_weight)
 
     quarter = width // NY
-    head_tiles = as_tiles(head_input)
-    size = head_tiles.shape[0]
+    shared = jnp.concatenate(
+        [
+            head_input.reshape(own_rows, 2, -1, 128).transpose(2, 1, 0, 3).reshape(-1, 128),
+            (tile_ids // RADIX).astype(jnp.bfloat16).reshape(-1, 128),
+            (tile_ids % RADIX).astype(jnp.bfloat16).reshape(-1, 128),
+            tile_probs.reshape(-1, 128),
+        ],
+        axis=0,
+    )
+    size, whole = own_rows * width // 128, shared.shape[0]
     packed = jnp.concatenate(
-        [replicate(head_tiles, NY), as_tiles(body_input).reshape(NY, -1, 128)], axis=1
+        [replicate(shared, NY), as_tiles(body_input).reshape(NY, -1, 128)], axis=1
     )
     packed = jnp.broadcast_to(packed[:, None], (NY, NZ) + packed.shape[1:])
     packed = packed.reshape((shards,) + packed.shape[2:])
     arrived = exchange(packed)
-    head_rows = from_tiles(arrived[:, :size], own_rows)
-    body_rows = swap_xy(from_tiles(arrived[:, size:], own_rows))
-
-    tile = jnp.concatenate(
-        [
-            (tile_ids // RADIX).astype(jnp.bfloat16),
-            (tile_ids % RADIX).astype(jnp.bfloat16),
-            tile_probs,
-        ],
-        axis=1,
-    )
-    store, source = collect(tile)
-    store = store.reshape(shards * slots, 3 * entries)
-    store_slot = (source[:, None] * slots + jnp.arange(slots, dtype=jnp.int32)).reshape(1, -1)
-    chosen_slot = (tile_slot[:, None] == store_slot).astype(jnp.bfloat16)
+    body_rows = from_tiles(swap_xy(arrived[:, whole:]), own_rows)
+    store = (
+        arrived[:, size:whole]
+        .reshape(shards, 3, slots, entries)
+        .transpose(0, 2, 1, 3)
+        .reshape(shards * slots, 3 * entries)
+    )
+    chosen_slot = (
+        tile_slot[:, None] == lax.broadcasted_iota(jnp.int32, (count, shards * slots), 1)
+    ).astype(jnp.bfloat16)
     found = jnp.dot(chosen_slot, store, preferred_element_type=jnp.float32)
     row_ids = (found[:, :entries] * RADIX + found[:, entries : 2 * entries]).astype(jnp.int32)
     row_probs = found[:, 2 * entries :]
     tail_mass = 1.0 - jnp.sum(row_probs, axis=1, keepdims=True)
-    marks = make_marks(row_ids - place * vocab, row_probs, vocab)
+    logits, marks = score(arrived, head_weight, row_ids - place * vocab, row_probs)
+    logits = logits.reshape(count, vocab)
     picked = marks >= 0.0
     teacher = jnp.maximum(marks, 0.0)
 
-    logits = jnp.einsum("rd,vd->rv", head_rows, head_weight, preferred_element_type=jnp.float32)
     local_max = jnp.max(logits, axis=1, keepdims=True)
     rest = jnp.where(picked, -1e30, logits)
     local_rest_max = jnp.max(rest, axis=1, keepdims=True)
@@ -306,20 +330,28 @@
         )
     ).astype(jnp.bfloat16)
 
-    parts = wide(body_rows, gate_full, 0)
-    parts = wide(body_rows, up_full, 1, parts)
+    acts = wide(body_rows, gate_full, 0, 2)
+    acts = wide(body_rows, up_full, 1, 2, acts)
+    chip = lax.axis_index("dp") // CORES
+
+    def turn_acts(step):
+        block = lax.dynamic_index_in_dim(acts, (chip + step) % NX, 0, keepdims=False)
+        return lax.ppermute(block, "dp", X_TURNS[step]) if step else block
+
+    gathered = [turn_acts(step) for step in range(NX)]
+    gate_act, up_act = sum(block.astype(jnp.float32) for block in gathered)
 
     partial = head_blocks(logit_grad, head_weight).reshape(NY, NZ, count, share)
     arrived = exchange(partial, Y_GROUPS)
     over_y = add_blocks(arrived).astype(jnp.bfloat16)
-    head_own = add_blocks(exchange(over_y, Z_GROUPS)).astype(jnp.bfloat16)
+    arrived = exchange(over_y, Z_GROUPS)
+    head_own = add_blocks(arrived).astype(jnp.bfloat16)
     head_own = swap_xy(head_own)
     head_grad = (
         exchange(replicate(head_own, NZ), Z_GROUPS).transpose(1, 0, 2).reshape(count, quarter)
     )
 
-    parts = wide(head_grad, down_full, 2, parts)
-    gate_act, up_act, down_grad = add_blocks(exchange(parts, X_GROUPS, "dp"))
+    down_grad = add_blocks(exchange(wide(head_grad, down_full, 0, 1)[:, 0], X_GROUPS, "dp"))
     sigma = 1.0 / (1.0 + jnp.exp(-gate_act))
     gate_grad = (down_grad * up_act * sigma * (1.0 + gate_act * (1.0 - sigma))).astype(jnp.bfloat16)
     up_grad = (down_grad * gate_act * sigma).astype(jnp.bfloat16)

time: 348 us -> 322 us (0.925)
  blocking collectives: 141 us -> 98 us
  waiting for transfers between devices: 82.7 us -> 102 us
  matrix products: 7.03 us -> 0.22 us
    all_to_all x2 -> x3, waiting for transfers between devices: 10.2 us -> 72.7 us  [exchange(): return lax.all_to_all(blocks, axis, 0, 0, axis_index_groups=groups)]
    ppermute x7 -> x3, waiting for transfers between devices: 60.7 us -> 0.01 us  [turn_acts(): return lax.ppermute(block, 'dp', X_TURNS[step]) if step else block]
    all_to_all x6 -> x5, blocking collectives: 141 us -> 98 us  [exchange(): return lax.all_to_all(blocks, axis, 0, 0, axis_index_groups=groups)]
    ppermute x3, waiting for transfers between devices: 9.68 us -> 26.8 us  [swap_xy(): return lax.ppermute(array, ('dp', 'vocab'), SWAP_XY)]
    dot_general x1 -> x0, matrix products: 6.81 us -> none  [layers(): jnp.einsum('rd,vd->rv', head_rows, head_weight, preferred_element_type=jn...]
    ppermute x3, starting transfers between devices: 12.3 us -> 7.96 us  [swap_xy(): return lax.ppermute(array, ('dp', 'vocab'), SWAP_XY)]
    all_to_all x2 -> x3, starting transfers between devices: 15.8 us -> 18.6 us  [exchange(): return lax.all_to_all(blocks, axis, 0, 0, axis_index_groups=groups)]
    ppermute x7 -> x3, starting transfers between devices: 14.1 us -> 13 us  [turn_acts(): return lax.ppermute(block, 'dp', X_TURNS[step]) if step else block]
  transfers between devices with their start and end apart: 15 -> 12, of which waited for: 8 -> 5; matrix products, arithmetic and copies ran while one was open for 5% -> 5% of each run, Pallas kernels for 8% -> 12%
where the time goes in v3:
time: 322 us; the launch traced here: 318 us
  waiting for transfers between devices  102 us (32%)
  blocking collectives  98 us (30%)
  Pallas kernels  47 us (15%)
  starting transfers between devices  39.6 us (12%)
  between operations  13.5 us (4%)
  local copies, waits for them, and re-layouts  10 us (3%)
  other arithmetic  7.75 us (2%)
    all_to_all x5, blocking collectives, exchange(): return lax.all_to_all(blocks, axis, 0, 0, axis_index_groups=groups)  98 us
    all_to_all x3, waiting for transfers between devices, exchange(): return lax.all_to_all(blocks, axis, 0, 0, axis_index_groups=groups)  72.7 us
    ppermute x3, waiting for transfers between devices, swap_xy(): return lax.ppermute(array, ('dp', 'vocab'), SWAP_XY)  26.8 us
    all_to_all x3, starting transfers between devices, exchange(): return lax.all_to_all(blocks, axis, 0, 0, axis_index_groups=groups)  18.6 us
    pallas_call x3, Pallas kernels, wide(): pl.pallas_call(wide_kernel, grid=(parts,), in_specs=in_specs, out_specs=p...  17.6 us
    ppermute x3, starting transfers between devices, turn_acts(): return lax.ppermute(block, 'dp', X_TURNS[step]) if step else block  13 us
    pallas_call x1, Pallas kernels, score(): pl.pallas_call(score_kernel, grid=(steps,), in_specs=[pl.BlockSpec((shard...  11.3 us
    pallas_call x1, Pallas kernels, branch_blocks(): pl.pallas_call(branch_kernel, grid=(NZ,), in_specs=[pl.BlockSpec(acts.sha...  10 us
  transfers between devices with their start and end apart: 12, of which 5 were waited for; matrix products, arithmetic and copies ran while one was open for 5% of the time, Pallas kernels for 12%

profile of v3, /device:TPU:2, one launch (start us, length us, event | category | flops | bytes accessed | tf_op | source)
XLA Modules:
  0.0 317.7 jit_solution(15080977197214744539)
XLA Ops:
  11.7 11.6 %all-to-all-start = ((bf16[32,344,128]{2,1,0:T(8,128)(2,1)}), bf16[32,344,128]{2,1,0:T(8,128)(2,1)S(1)}, u32[]{:S(2)}, u32[]{:S(2)}) async-start(bf16[32,344,128]{2,1,0:T(8,128)(2,1)} %bitcast.68), calls=%async_computation | async-start | bytes 5636096 | tf_op jit(solution)/shard_map/all_to_all | solution.py:41
  23.3 67.6 %all-to-all-done.blocks_ref = bf16[32,344,128]{2,1,0:T(8,128)(2,1)S(1)} async-done(((bf16[32,344,128]{2,1,0:T(8,128)(2,1)}), bf16[32,344,128]{2,1,0:T(8,128)(2,1)S(1)}, u32[]{:S(2)}, u32[]{:S(2)}) %all-to-all-start) | async-done | bytes 2818080 | tf_op jit(solution)/shard_map/all_to_all | solution.py:41
  92.7 11.3 %score.1 = (f32[32,4,512]{2,1,0:T(4,128)}, f32[128,512]{1,0:T(8,128)}) custom-call(bf16[32,344,128]{2,1,0:T(8,128)(2,1)} %copy-done, bf16[512,8192]{1,0:T(8,128)(2,1)} %weight_ref.1, bf16[512,8192]{1,0:T(8,128)(2,1)} %weight_ref.1, s32[128,128]{1,0:T(8,128)} %fusion.10.columns_ref, f32[128,128]{1,0:T(8,128)} %get-tuple-element.21.probs_ref), custom_call_target="tpu_custom_call" | custom-call | flops 1073741824 | bytes 8388608 | tf_op jit(solution)/shard_map/score/pallas_call | solution.py:216
  107.7 14.3 %all_to_all.40 = f32[32,4,128]{2,1,0:T(4,128)S(1)} all-to-all(f32[32,4,128]{2,1,0:T(4,128)S(1)} %broadcast_in_dim.61), channel_id=1, replica_groups=mesh['dp'=8,'vocab'=32] {'vocab'}, dimensions={0} | all-to-all | bytes 131072 | tf_op jit(solution)/shard_map/all_to_all | solution.py:41
  124.0 8.0 %head.1 = bf16[32,128,256]{2,1,0:T(8,128)(2,1)} custom-call(bf16[128,512]{1,0:T(8,128)(2,1)} %multiply_convert_fusion.grad_ref, bf16[512,8192]{1,0:T(8,128)(2,1)} %weight_ref.1), custom_call_target="tpu_custom_call" | custom-call | flops 1073741824 | bytes 8388608 | tf_op jit(solution)/shard_map/head/pallas_call | solution.py:157
  132.0 28.8 %all_to_all.41 = bf16[4,8,128,256]{3,2,1,0:T(8,128)(2,1)S(1)} all-to-all(bf16[4,8,128,256]{3,2,1,0:T(8,128)(2,1)} %bitcast.69), channel_id=1, replica_groups={{0,8,16,24},{1,9,17,25},{2,10,18,26},{3,11,19,27},{4,12,20,28},{5,13,21..., dimensions={0} | all-to-all | bytes 4194304 | tf_op jit(solution)/shard_map/all_to_all | solution.py:41
  161.2 21.5 %all_to_all.42 = bf16[8,128,256]{2,1,0:T(8,128)(2,1)S(1)} all-to-all(bf16[8,128,256]{2,1,0:T(8,128)(2,1)S(1)} %reduce_sum.94), channel_id=1, replica_groups={{0,1,2,3,4,5,6,7},{8,9,10,11,12,13,14,15},{16,17,18,19,20,21,22,23},{24..., dimensions={0} | all-to-all | bytes 1048576 | tf_op jit(solution)/shard_map/all_to_all | solution.py:41
  182.8 3.1 collective-permute-start
  185.9 4.1 %collective-permute-done = bf16[128,256]{1,0:T(8,128)(2,1)S(1)} collective-permute-done((bf16[128,256]{1,0:T(8,128)(2,1)S(1)}, bf16[128,256]{1,0:T(8,128)(2,1)S(1)}, u32[]{:S(2)}, u32[]{:S(2)}) %collective-permute-start) | collective-permute-done | bytes 65568 | tf_op jit(solution)/shard_map/ppermute | solution.py:45
  190.8 3.5 %all-to-all-start.4 = ((bf16[8,128,256]{2,1,0:T(8,128)(2,1)}), bf16[8,128,256]{2,1,0:T(8,128)(2,1)S(1)}, u32[]{:S(2)}, u32[]{:S(2)}) async-start(bf16[8,128,256]{2,1,0:T(8,128)(2,1)} %broadcast_in_dim.62), calls=%async_computation.4 | async-start | bytes 1048576 | tf_op jit(solution)/shard_map/all_to_all | solution.py:41
  195.4 3.0 collective-permute-start.1
  198.5 17.6 %collective-permute-done.1 = bf16[32,64,128]{2,1,0:T(8,128)(2,1)S(1)} collective-permute-done((bf16[32,64,128]{2,1,0:T(8,128)(2,1)S(1)}, bf16[32,64,128]{2,1,0:T(8,128)(2,1)S(1)}, u32[]{:S(2)}, u32[]{:S(2)}) %collective-permute-start.1) | collective-permute-done | bytes 524320 | tf_op jit(solution)/shard_map/ppermute | solution.py:45
  217.1 5.9 %wide.4.refs_0_ = bf16[4,2,448,128]{3,2,1,0:T(8,128)(2,1)} custom-call(bf16[128,2048]{1,0:T(8,128)(2,1)} %bitcast.71, bf16[8,448,1024]{2,1,0:T(8,128)(2,1)} %bitcast.64), custom_call_target="tpu_custom_call" | custom-call | flops 939524096 | bytes 7864320 | tf_op jit(solution)/shard_map/wide/pallas_call | solution.py:91
  223.0 5.9 %wide.5 = bf16[4,2,448,128]{3,2,1,0:T(8,128)(2,1)} custom-call(bf16[128,2048]{1,0:T(8,128)(2,1)} %bitcast.72, bf16[8,448,1024]{2,1,0:T(8,128)(2,1)} %bitcast.66, bf16[4,2,448,128]{3,2,1,0:T(8,128)(2,1)} %wide.4.refs_0_), custom_call_target="tpu_custom_call", output_to_operand_aliasing={{}: (2, {})} | custom-call | flops 939524096 | bytes 7864320 | tf_op jit(solution)/shard_map/wide/pallas_call | solution.py:91
  230.1 6.4 %collective-permute-start.2 = (bf16[2,448,128]{2,1,0:T(8,128)(2,1)S(1)}, bf16[2,448,128]{2,1,0:T(8,128)(2,1)S(1)}, u32[]{:S(2)}, u32[]{:S(2)}) collective-permute-start(bf16[2,448,128]{2,1,0:T(8,128)(2,1)S(1)} %get-tuple-element.15), channel_id=1, source_target_pairs={{0,64},{32,96},{64,128},{96,160},{128,192},{160,224},{192,0},{224,... | collective-permute-start | bytes 688136 | tf_op jit(solution)/shard_map/ppermute | solution.py:339
  236.4 4.1 %collective-permute-start.3 = (bf16[2,448,128]{2,1,0:T(8,128)(2,1)S(1)}, bf16[2,448,128]{2,1,0:T(8,128)(2,1)S(1)}, u32[]{:S(2)}, u32[]{:S(2)}) collective-permute-start(bf16[2,448,128]{2,1,0:T(8,128)(2,1)S(1)} %get-tuple-element.17), channel_id=1, source_target_pairs={{0,128},{32,160},{64,192},{96,224},{128,0},{160,32},{192,64},{224,... | collective-permute-start | bytes 688136 | tf_op jit(solution)/shard_map/ppermute | solution.py:339
  240.6 2.5 collective-permute-start.4
  244.0 5.9 %wide.3 = bf16[4,1,448,128]{3,2,1,0:T(8,128)(2,1)} custom-call(bf16[128,2048]{1,0:T(8,128)(2,1)} %bitcast.73, bf16[8,448,1024]{2,1,0:T(8,128)(2,1)} %bitcast.70), custom_call_target="tpu_custom_call" | custom-call | flops 939524096 | bytes 7864320 | tf_op jit(solution)/shard_map/wide/pallas_call | solution.py:91
  249.8 3.5 %all-to-all-start.5 = ((bf16[4,448,128]{2,1,0:T(8,128)(2,1)}), bf16[4,448,128]{2,1,0:T(8,128)(2,1)S(1)}, u32[]{:S(2)}, u32[]{:S(2)}) async-start(bf16[4,448,128]{2,1,0:T(8,128)(2,1)} %bitcast.76), calls=%async_computation.5 | async-start | bytes 917504 | tf_op jit(solution)/shard_map/all_to_all | solution.py:41
  254.4 5.1 %all-to-all-done.5 = bf16[4,448,128]{2,1,0:T(8,128)(2,1)S(1)} async-done(((bf16[4,448,128]{2,1,0:T(8,128)(2,1)}), bf16[4,448,128]{2,1,0:T(8,128)(2,1)S(1)}, u32[]{:S(2)}, u32[]{:S(2)}) %all-to-all-start.5) | async-done | bytes 458784 | tf_op jit(solution)/shard_map/all_to_all | solution.py:41
  259.9 13.3 %all_to_all.43.act_ref = bf16[4,2,448,128]{3,2,1,0:T(8,128)(2,1)} all-to-all(bf16[4,2,448,128]{3,2,1,0:T(8,128)(2,1)S(1)} %broadcast_in_dim.63), channel_id=1, replica_groups={{0,64,128,192},{32,96,160,224},{1,65,129,193},{33,97,161,225},{2,66,130..., dimensions={0} | all-to-all | bytes 1835008 | tf_op jit(solution)/shard_map/all_to_all | solution.py:41
  273.2 10.0 %branch.1 = bf16[8,128,256]{2,1,0:T(8,128)(2,1)} custom-call(bf16[4,2,448,128]{3,2,1,0:T(8,128)(2,1)} %all_to_all.43.act_ref, bf16[4,2,448,1024]{3,2,1,0:T(8,128)(2,1)} %bitcast.65, bf16[4,2,448,1024]{3,2,1,0:T(8,128)(2,1)} %bitcast.67), custom_call_target="tpu_custom_call" | custom-call | flops 1879048192 | bytes 14680064 | tf_op jit(solution)/shard_map/branch/pallas_call | solution.py:126
  283.2 20.1 %all_to_all.44 = bf16[8,128,256]{2,1,0:T(8,128)(2,1)S(1)} all-to-all(bf16[8,128,256]{2,1,0:T(8,128)(2,1)} %branch.1), channel_id=1, replica_groups={{0,1,2,3,4,5,6,7},{8,9,10,11,12,13,14,15},{16,17,18,19,20,21,22,23},{24..., dimensions={0} | all-to-all | bytes 1048576 | tf_op jit(solution)/shard_map/all_to_all | solution.py:41
  305.4 5.1 %collective-permute-done.5 = bf16[128,256]{1,0:T(8,128)(2,1)S(1)} collective-permute-done((bf16[128,256]{1,0:T(8,128)(2,1)S(1)}, bf16[128,256]{1,0:T(8,128)(2,1)S(1)}, u32[]{:S(2)}, u32[]{:S(2)}) %collective-permute-start.5) | collective-permute-done | bytes 65568 | tf_op jit(solution)/shard_map/ppermute | solution.py:45
  (64 shorter events, 22.1 us)
Async XLA Ops:
  6.5 3.1 copy-start.2
  6.5 3.2 copy-start.3
  6.5 3.2 %copy-start.1 = (bf16[4,8192]{1,0:T(4,128)(2,1)S(1)}, bf16[4,8192]{1,0:T(4,128)(2,1)}, u32[]{:S(2)}) copy-start(bf16[4,8192]{1,0:T(4,128)(2,1)} %param.10) | copy-start | bytes 196612
  6.5 210.6 %all-gather.11.cloned.1.call-start = ((), (), s32[]{:S(2)}) async-start(), calls=%async_computation.10 | async-start | bytes 8257536 | tf_op jit(solution)/shard_map/all_gather | solution.py:243
  7.3 215.7 %all-gather.9.cloned.1.call-start = ((), (), s32[]{:S(2)}) async-start(), calls=%async_computation.9 | async-start | bytes 8257536 | tf_op jit(solution)/shard_map/all_gather | solution.py:243
  8.0 236.0 %all-gather.7.cloned.1.call-start = ((), (), s32[]{:S(2)}) async-start(), calls=%async_computation.8 | async-start | bytes 8257536 | tf_op jit(solution)/shard_map/all_gather | solution.py:243
  11.7 79.2 %copy-start.4 = (s32[128]{0:T(128)S(1)}, s32[128]{0:T(128)}, u32[]{:S(2)}) copy-start(s32[128]{0:T(128)} %param.17) | copy-start | bytes 1540
  11.7 79.2 %all-to-all-start = ((bf16[32,344,128]{2,1,0:T(8,128)(2,1)}), bf16[32,344,128]{2,1,0:T(8,128)(2,1)S(1)}, u32[]{:S(2)}, u32[]{:S(2)}) async-start(bf16[32,344,128]{2,1,0:T(8,128)(2,1)} %bitcast.68), calls=%async_computation | async-start | bytes 5636096 | tf_op jit(solution)/shard_map/all_to_all | solution.py:41
  90.9 1.8 copy-start
  182.8 7.2 %collective-permute-start = (bf16[128,256]{1,0:T(8,128)(2,1)S(1)}, bf16[128,256]{1,0:T(8,128)(2,1)S(1)}, u32[]{:S(2)}, u32[]{:S(2)}) collective-permute-start(bf16[128,256]{1,0:T(8,128)(2,1)S(1)} %reduce_sum.95), channel_id=1, source_target_pairs={{0,0},{1,1},{2,2},{3,3},{4,4},{5,5},{6,6},{7,7},{8,64},{9,65},{10,... | collective-permute-start | bytes 196616 | tf_op jit(solution)/shard_map/ppermute | solution.py:45
  190.8 52.3 %all-to-all-start.4 = ((bf16[8,128,256]{2,1,0:T(8,128)(2,1)}), bf16[8,128,256]{2,1,0:T(8,128)(2,1)S(1)}, u32[]{:S(2)}, u32[]{:S(2)}) async-start(bf16[8,128,256]{2,1,0:T(8,128)(2,1)} %broadcast_in_dim.62), calls=%async_computation.4 | async-start | bytes 1048576 | tf_op jit(solution)/shard_map/all_to_all | solution.py:41
  195.4 20.6 %collective-permute-start.1 = (bf16[32,64,128]{2,1,0:T(8,128)(2,1)S(1)}, bf16[32,64,128]{2,1,0:T(8,128)(2,1)S(1)}, u32[]{:S(2)}, u32[]{:S(2)}) collective-permute-start(bf16[32,64,128]{2,1,0:T(8,128)(2,1)S(1)} %slice.24), channel_id=1, source_target_pairs={{0,0},{1,1},{2,2},{3,3},{4,4},{5,5},{6,6},{7,7},{8,64},{9,65},{10,... | collective-permute-start | bytes 1572872 | tf_op jit(solution)/shard_map/ppermute | solution.py:45
  230.1 23.3 %collective-permute-start.2 = (bf16[2,448,128]{2,1,0:T(8,128)(2,1)S(1)}, bf16[2,448,128]{2,1,0:T(8,128)(2,1)S(1)}, u32[]{:S(2)}, u32[]{:S(2)}) collective-permute-start(bf16[2,448,128]{2,1,0:T(8,128)(2,1)S(1)} %get-tuple-element.15), channel_id=1, source_target_pairs={{0,64},{32,96},{64,128},{96,160},{128,192},{160,224},{192,0},{224,... | collective-permute-start | bytes 688136 | tf_op jit(solution)/shard_map/ppermute | solution.py:339
  236.4 16.9 %collective-permute-start.3 = (bf16[2,448,128]{2,1,0:T(8,128)(2,1)S(1)}, bf16[2,448,128]{2,1,0:T(8,128)(2,1)S(1)}, u32[]{:S(2)}, u32[]{:S(2)}) collective-permute-start(bf16[2,448,128]{2,1,0:T(8,128)(2,1)S(1)} %get-tuple-element.17), channel_id=1, source_target_pairs={{0,128},{32,160},{64,192},{96,224},{128,0},{160,32},{192,64},{224,... | collective-permute-start | bytes 688136 | tf_op jit(solution)/shard_map/ppermute | solution.py:339
  240.6 12.8 %collective-permute-start.4 = (bf16[2,448,128]{2,1,0:T(8,128)(2,1)S(1)}, bf16[2,448,128]{2,1,0:T(8,128)(2,1)S(1)}, u32[]{:S(2)}, u32[]{:S(2)}) collective-permute-start(bf16[2,448,128]{2,1,0:T(8,128)(2,1)S(1)} %get-tuple-element.16), channel_id=1, source_target_pairs={{0,192},{32,224},{64,0},{96,32},{128,64},{160,96},{192,128},{224,1... | collective-permute-start | bytes 688136 | tf_op jit(solution)/shard_map/ppermute | solution.py:339
  249.8 9.7 %all-to-all-start.5 = ((bf16[4,448,128]{2,1,0:T(8,128)(2,1)}), bf16[4,448,128]{2,1,0:T(8,128)(2,1)S(1)}, u32[]{:S(2)}, u32[]{:S(2)}) async-start(bf16[4,448,128]{2,1,0:T(8,128)(2,1)} %bitcast.76), calls=%async_computation.5 | async-start | bytes 917504 | tf_op jit(solution)/shard_map/all_to_all | solution.py:41
  303.5 7.1 %collective-permute-start.5 = (bf16[128,256]{1,0:T(8,128)(2,1)S(1)}, bf16[128,256]{1,0:T(8,128)(2,1)S(1)}, u32[]{:S(2)}, u32[]{:S(2)}) collective-permute-start(bf16[128,256]{1,0:T(8,128)(2,1)S(1)} %add_convert_fusion), channel_id=1, source_target_pairs={{0,0},{1,1},{2,2},{3,3},{4,4},{5,5},{6,6},{7,7},{8,64},{9,65},{10,... | collective-permute-start | bytes 196616 | tf_op jit(solution)/shard_map/ppermute | solution.py:45
Sparse Core Ops, SparseCore 0:
  9.2 77.9 all-gather.10
  89.0 48.6 all-gather.8
  139.5 52.9 all-gather.6

commit v4 on v3

--- a/solution.py
+++ b/solution.py
@@ -23,26 +23,21 @@
     step: [(x * CORES + c, (x + step) % NX * CORES + c) for x in range(NX) for c in range(CORES)]
     for step in range(1, NX)
 }
-SWAP_XY = [
-    (
-        (x * CORES + c) * NY * NZ + y * NZ + z,
-        (y * CORES + c) * NY * NZ + x * NZ + z,
-    )
-    for x in range(NX)
+XZ_GROUPS = [
+    [(x * CORES + c) * NY * NZ + y * NZ + z for x in range(NX) for z in range(NZ)]
     for c in range(CORES)
     for y in range(NY)
-    for z in range(NZ)
 ]
+X_TURNS = {
+    step: [(x * CORES + c, (x + step) % NX * CORES + c) for x in range(NX) for c in range(CORES)]
+    for step in range(1, NX)
+}
 NT = (((1,), (1,)), ((), ()))
 TN = (((0,), (0,)), ((), ()))
 
 
 def exchange(blocks, groups=None, axis="vocab"):
     return lax.all_to_all(blocks, axis, 0, 0, axis_index_groups=groups)
-
-
-def swap_xy(array):
-    return lax.ppermute(array, ("dp", "vocab"), SWAP_XY)
 
 
 def replicate(block, copies):
@@ -104,7 +99,7 @@
     )(*args)
 
 
-def branch_kernel(act_ref, gate_weight_ref, up_weight_ref, out_ref):
+def branch_kernel(place_ref, act_ref, gate_weight_ref, up_weight_ref, extra_ref, out_ref):
     total = None
     for i in range(act_ref.shape[0]):
         for k, weight in enumerate((gate_weight_ref, up_weight_ref)):
@@ -112,10 +107,12 @@
                 act_ref[i, k], weight[i, 0], TN, preferred_element_type=jnp.float32
             )
             total = part if total is None else total + part
-    out_ref[0] = total.astype(out_ref.dtype)
-
-
-def branch_blocks(acts, gate_weight, up_weight):
+    total += jnp.where(pl.program_id(0) == place_ref[0], extra_ref[...].astype(jnp.float32), 0.0)
+    parts, _, rows, share = out_ref.shape
+    out_ref[:, 0] = total.reshape(parts, rows, share).astype(out_ref.dtype)
+
+
+def branch_blocks(acts, gate_weight, up_weight, extra, place):
     parts, _, hidden, count = acts.shape
     half = gate_weight.shape[2]
     share = CORES * half // NZ
@@ -126,32 +123,39 @@
     return pl.pallas_call(
         branch_kernel,
         grid=(NZ,),
-        in_specs=[pl.BlockSpec(acts.shape, lambda i: (0, 0, 0, 0)), weight_spec, weight_spec],
-        out_specs=pl.BlockSpec((1, count, share), lambda i: (i, 0, 0)),
-        out_shape=jax.ShapeDtypeStruct((NZ, count, share), jnp.bfloat16),
+        in_specs=[
+            pl.BlockSpec(memory_space=pltpu.SMEM),
+            pl.BlockSpec(acts.shape, lambda i: (0, 0, 0, 0)),
+            weight_spec,
+            weight_spec,
+            pl.BlockSpec(extra.shape, lambda i: (0, 0)),
+        ],
+        out_specs=pl.BlockSpec((NX, 1, count // NX, share), lambda i: (0, i, 0, 0)),
+        out_shape=jax.ShapeDtypeStruct((NX, NZ, count // NX, share), jnp.bfloat16),
         cost_estimate=pl.CostEstimate(
             flops=4 * count * gate_weight.size,
             bytes_accessed=4 * gate_weight.size,
             transcendentals=0,
         ),
         name="branch",
-    )(acts, gate_weight, up_weight)
+    )(place, acts, gate_weight, up_weight, extra)
 
 
 def head_kernel(grad_ref, weight_ref, out_ref):
-    for i in range(out_ref.shape[0]):
-        share = out_ref.shape[2]
-        out_ref[i] = jnp.dot(
+    quarters, steps, rows, share = out_ref.shape
+    for i in range(steps):
+        part = jnp.dot(
             grad_ref[...],
             weight_ref[:, i * share : (i + 1) * share],
             preferred_element_type=jnp.float32,
-        ).astype(out_ref.dtype)
+        )
+        out_ref[:, i] = part.reshape(quarters, rows, share).astype(out_ref.dtype)
 
 
 def head_blocks(grad, weight):
     count, vocab = grad.shape
     width = weight.shape[1]
-    parts = NY * NZ
+    parts = NX * NZ
     share = width // parts
     step = 4
     return pl.pallas_call(
@@ -161,8 +165,8 @@
             pl.BlockSpec(grad.shape, lambda i: (0, 0)),
             pl.BlockSpec((vocab, step * share), lambda i: (0, i)),
         ],
-        out_specs=pl.BlockSpec((step, count, share), lambda i: (i, 0, 0)),
-        out_shape=jax.ShapeDtypeStruct((parts, count, share), jnp.bfloat16),
+        out_specs=pl.BlockSpec((NY, step, count // NY, share), lambda i: (0, i, 0, 0)),
+        out_shape=jax.ShapeDtypeStruct((NY, parts, count // NY, share), jnp.bfloat16),
         cost_estimate=pl.CostEstimate(
             flops=2 * count * weight.size,
             bytes_accessed=2 * weight.size,
@@ -266,8 +270,8 @@
     up_full = gather_weight(up_weight)
     down_full = gather_weight(down_weight)
 
-    quarter = width // NY
-    shared = jnp.concatenate(
+    quarter = width // NX
+    packed = jnp.concatenate(
         [
             head_input.reshape(own_rows, 2, -1, 128).transpose(2, 1, 0, 3).reshape(-1, 128),
             (tile_ids // RADIX).astype(jnp.bfloat16).reshape(-1, 128),
@@ -276,14 +280,15 @@
         ],
         axis=0,
     )
-    size, whole = own_rows * width // 128, shared.shape[0]
-    packed = jnp.concatenate(
-        [replicate(shared, NY), as_tiles(body_input).reshape(NY, -1, 128)], axis=1
-    )
-    packed = jnp.broadcast_to(packed[:, None], (NY, NZ) + packed.shape[1:])
-    packed = packed.reshape((shards,) + packed.shape[2:])
-    arrived = exchange(packed)
-    body_rows = from_tiles(swap_xy(arrived[:, whole:]), own_rows)
+    size, whole = own_rows * width // 128, packed.shape[0]
+    arrived = exchange(replicate(packed, shards))
+
+    body_tiles = as_tiles(body_input).reshape(NX, 1, -1, 128)
+    body_tiles = jnp.broadcast_to(body_tiles, (NX, NZ) + body_tiles.shape[2:])
+    body_tiles = exchange(
+        body_tiles.reshape((NX * NZ,) + body_tiles.shape[2:]), XZ_GROUPS, ("dp", "vocab")
+    )
+    body_rows = from_tiles(body_tiles, own_rows)
     store = (
         arrived[:, size:whole]
         .reshape(shards, 3, slots, entries)
@@ -341,12 +346,13 @@
     gathered = [turn_acts(step) for step in range(NX)]
     gate_act, up_act = sum(block.astype(jnp.float32) for block in gathered)
 
-    partial = head_blocks(logit_grad, head_weight).reshape(NY, NZ, count, share)
-    arrived = exchange(partial, Y_GROUPS)
+    arrived = exchange(head_blocks(logit_grad, head_weight), Y_GROUPS)
     over_y = add_blocks(arrived).astype(jnp.bfloat16)
-    arrived = exchange(over_y, Z_GROUPS)
-    head_own = add_blocks(arrived).astype(jnp.bfloat16)
-    head_own = swap_xy(head_own)
+    arrived = exchange(over_y, XZ_GROUPS, ("dp", "vocab"))
+    head_own = jnp.sum(
+        arrived.reshape((NX, NZ) + arrived.shape[1:]).astype(jnp.float32), axis=1
+    ).astype(jnp.bfloat16)
+    head_own = head_own.reshape(count, share)
     head_grad = (
         exchange(replicate(head_own, NZ), Z_GROUPS).transpose(1, 0, 2).reshape(count, quarter)
     )
@@ -356,8 +362,12 @@
     gate_grad = (down_grad * up_act * sigma * (1.0 + gate_act * (1.0 - sigma))).astype(jnp.bfloat16)
     up_grad = (down_grad * gate_act * sigma).astype(jnp.bfloat16)
     both = exchange(replicate(jnp.stack([gate_grad, up_grad]), NX), X_GROUPS, "dp")
-    summed = add_blocks(exchange(branch_blocks(both, gate_full, up_full), Z_GROUPS))
-    return swap_xy((head_own.astype(jnp.float32) + summed).astype(jnp.bfloat16))
+    pieces = branch_blocks(both, gate_full, up_full, head_own, (place % NZ).reshape(1))
+    arrived = exchange(
+        pieces.reshape((NX * NZ,) + pieces.shape[2:]), XZ_GROUPS, ("dp", "vocab")
+    )
+    grads = jnp.sum(arrived.reshape((NX, NZ) + arrived.shape[1:]).astype(jnp.float32), axis=1)
+    return exchange(grads.astype(jnp.bfloat16), Y_GROUPS).reshape(count, share)
 
 
 def solution(mesh):

time: 322 us -> 309 us (0.960)
  waiting for transfers between devices: 102 us -> 87.8 us
  blocking collectives: 98 us -> 102 us
    ppermute x3 -> x0, waiting for transfers between devices: 26.8 us -> none  [swap_xy(): return lax.ppermute(array, ('dp', 'vocab'), SWAP_XY)]
    all_to_all x3 -> x5, starting transfers between devices: 18.6 us -> 33 us  [exchange(): return lax.all_to_all(blocks, axis, 0, 0, axis_index_groups=groups)]
    all_to_all x3 -> x5, waiting for transfers between devices: 72.7 us -> 85.7 us  [exchange(): return lax.all_to_all(blocks, axis, 0, 0, axis_index_groups=groups)]
    ppermute x3, starting transfers between devices: 13 us -> 4.08 us  [turn_acts(): return lax.ppermute(block, 'dp', X_TURNS[step]) if step else block]
    ppermute x3 -> x0, starting transfers between devices: 7.96 us -> none  [swap_xy(): return lax.ppermute(array, ('dp', 'vocab'), SWAP_XY)]
    all_to_all x5, blocking collectives: 98 us -> 102 us  [exchange(): return lax.all_to_all(blocks, axis, 0, 0, axis_index_groups=groups)]
  transfers between devices with their start and end apart: 12 -> 11, of which waited for: 5 -> 4; matrix products, arithmetic and copies ran while one was open for 5% -> 5% of each run, Pallas kernels for 12% -> 12%
where the time goes in v4:
time: 309 us; the launch traced here: 306 us
  blocking collectives  102 us (33%)
  waiting for transfers between devices  87.8 us (28%)
  Pallas kernels  47.1 us (15%)
  starting transfers between devices  37.2 us (12%)
  between operations  13.3 us (4%)
  local copies, waits for them, and re-layouts  11.3 us (4%)
  other arithmetic  6.87 us (2%)
    all_to_all x5, blocking collectives, exchange(): return lax.all_to_all(blocks, axis, 0, 0, axis_index_groups=groups)  102 us
    all_to_all x5, waiting for transfers between devices, exchange(): return lax.all_to_all(blocks, axis, 0, 0, axis_index_groups=groups)  85.7 us
    all_to_all x5, starting transfers between devices, exchange(): return lax.all_to_all(blocks, axis, 0, 0, axis_index_groups=groups)  33 us
    pallas_call x3, Pallas kernels, wide(): pl.pallas_call(wide_kernel, grid=(parts,), in_specs=in_specs, out_specs=p...  17.6 us
    pallas_call x1, Pallas kernels, score(): pl.pallas_call(score_kernel, grid=(steps,), in_specs=[pl.BlockSpec((shard...  11.1 us
    pallas_call x1, Pallas kernels, branch_blocks(): pl.pallas_call(branch_kernel, grid=(NZ,), in_specs=[pl.BlockSpec(memory_s...  10.1 us
    pallas_call x1, Pallas kernels, head_blocks(): pl.pallas_call(head_kernel, grid=(parts // step,), in_specs=[pl.BlockSpec...  8.24 us
  transfers between devices with their start and end apart: 11, of which 4 were waited for; matrix products, arithmetic and copies ran while one was open for 5% of the time, Pallas kernels for 12%

profile of v4, /device:TPU:2, one launch (start us, length us, event | category | flops | bytes accessed | tf_op | source)
XLA Modules:
  0.0 306.0 jit_solution(2040447750159731989)
XLA Ops:
  8.9 1.7 broadcast_in_dim.56
  10.6 11.6 %all-to-all-start = ((bf16[32,280,128]{2,1,0:T(8,128)(2,1)}), bf16[32,280,128]{2,1,0:T(8,128)(2,1)S(1)}, u32[]{:S(2)}, u32[]{:S(2)}) async-start(bf16[32,280,128]{2,1,0:T(8,128)(2,1)} %broadcast_in_dim.56), calls=%async_computation | async-start | bytes 4587520 | tf_op jit(solution)/shard_map/all_to_all | solution.py:40
  22.3 56.5 %all-to-all-done.blocks_ref = bf16[32,280,128]{2,1,0:T(8,128)(2,1)S(1)} async-done(((bf16[32,280,128]{2,1,0:T(8,128)(2,1)}), bf16[32,280,128]{2,1,0:T(8,128)(2,1)S(1)}, u32[]{:S(2)}, u32[]{:S(2)}) %all-to-all-start) | async-done | bytes 2293792 | tf_op jit(solution)/shard_map/all_to_all | solution.py:40
  80.5 11.1 %score.1 = (f32[32,4,512]{2,1,0:T(4,128)}, f32[128,512]{1,0:T(8,128)}) custom-call(bf16[32,280,128]{2,1,0:T(8,128)(2,1)} %copy-done, bf16[512,8192]{1,0:T(8,128)(2,1)} %weight_ref.1, bf16[512,8192]{1,0:T(8,128)(2,1)} %weight_ref.1, s32[128,128]{1,0:T(8,128)} %fusion.10.columns_ref, f32[128,128]{1,0:T(8,128)} %get-tuple-element.21.probs_ref), custom_call_target="tpu_custom_call" | custom-call | flops 1073741824 | bytes 8388608 | tf_op jit(solution)/shard_map/score/pallas_call | solution.py:220
  94.0 1.1 fusion.8
  95.4 13.9 %all_to_all.50 = f32[32,4,128]{2,1,0:T(4,128)S(1)} all-to-all(f32[32,4,128]{2,1,0:T(4,128)S(1)} %broadcast_in_dim.62), channel_id=1, replica_groups=mesh['dp'=8,'vocab'=32] {'vocab'}, dimensions={0} | all-to-all | bytes 131072 | tf_op jit(solution)/shard_map/all_to_all | solution.py:40
  110.4 8.2 %head.1 = bf16[4,32,32,256]{3,2,1,0:T(8,128)(2,1)} custom-call(bf16[128,512]{1,0:T(8,128)(2,1)} %multiply_convert_fusion.grad_ref, bf16[512,8192]{1,0:T(8,128)(2,1)} %weight_ref.1), custom_call_target="tpu_custom_call" | custom-call | flops 1073741824 | bytes 8388608 | tf_op jit(solution)/shard_map/head/pallas_call | solution.py:161
  118.6 34.4 %all_to_all.51 = bf16[4,32,32,256]{3,2,1,0:T(8,128)(2,1)S(1)} all-to-all(bf16[4,32,32,256]{3,2,1,0:T(8,128)(2,1)} %head.1), channel_id=1, replica_groups={{0,8,16,24},{1,9,17,25},{2,10,18,26},{3,11,19,27},{4,12,20,28},{5,13,21..., dimensions={0} | all-to-all | bytes 4194304 | tf_op jit(solution)/shard_map/all_to_all | solution.py:40
  153.4 24.9 %all_to_all.52 = bf16[32,32,256]{2,1,0:T(8,128)(2,1)S(1)} all-to-all(bf16[32,32,256]{2,1,0:T(8,128)(2,1)S(1)} %reduce_sum.97), channel_id=1, replica_groups={{0,1,2,3,4,5,6,7,64,65,66,67,68,69,70,71,128,129,130,131,132,133,134,13..., dimensions={0} | all-to-all | bytes 1048576 | tf_op jit(solution)/shard_map/all_to_all | solution.py:40
  179.2 7.0 %all-to-all-start.6 = ((bf16[32,64,128]{2,1,0:T(8,128)(2,1)}), bf16[32,64,128]{2,1,0:T(8,128)(2,1)S(1)}, u32[]{:S(2)}, u32[]{:S(2)}) async-start(bf16[32,64,128]{2,1,0:T(8,128)(2,1)} %bitcast.20), calls=%async_computation.6 | async-start | bytes 1048576 | tf_op jit(solution)/shard_map/all_to_all | solution.py:40
  186.4 14.6 %all-to-all-done.6 = bf16[32,64,128]{2,1,0:T(8,128)(2,1)S(1)} async-done(((bf16[32,64,128]{2,1,0:T(8,128)(2,1)}), bf16[32,64,128]{2,1,0:T(8,128)(2,1)S(1)}, u32[]{:S(2)}, u32[]{:S(2)}) %all-to-all-start.6) | async-done | bytes 524320 | tf_op jit(solution)/shard_map/all_to_all | solution.py:40
  201.8 4.6 %all-to-all-start.4 = ((bf16[8,128,256]{2,1,0:T(8,128)(2,1)}), bf16[8,128,256]{2,1,0:T(8,128)(2,1)S(1)}, u32[]{:S(2)}, u32[]{:S(2)}) async-start(bf16[8,128,256]{2,1,0:T(8,128)(2,1)} %broadcast_in_dim.64), calls=%async_computation.4 | async-start | bytes 1048576 | tf_op jit(solution)/shard_map/all_to_all | solution.py:40
  208.0 5.9 %wide.4.refs_0_ = bf16[4,2,448,128]{3,2,1,0:T(8,128)(2,1)} custom-call(bf16[128,2048]{1,0:T(8,128)(2,1)} %bitcast.77, bf16[8,448,1024]{2,1,0:T(8,128)(2,1)} %bitcast.74), custom_call_target="tpu_custom_call" | custom-call | flops 939524096 | bytes 7864320 | tf_op jit(solution)/shard_map/wide/pallas_call | solution.py:86
  213.9 5.9 %wide.5 = bf16[4,2,448,128]{3,2,1,0:T(8,128)(2,1)} custom-call(bf16[128,2048]{1,0:T(8,128)(2,1)} %bitcast.78, bf16[8,448,1024]{2,1,0:T(8,128)(2,1)} %bitcast.72, bf16[4,2,448,128]{3,2,1,0:T(8,128)(2,1)} %wide.4.refs_0_), custom_call_target="tpu_custom_call", output_to_operand_aliasing={{}: (2, {})} | custom-call | flops 939524096 | bytes 7864320 | tf_op jit(solution)/shard_map/wide/pallas_call | solution.py:86
  219.8 1.2 dynamic-slice_bitcast_fusion.2
  221.8 2.8 collective-permute-start.1
  226.0 5.9 %wide.3 = bf16[4,1,448,128]{3,2,1,0:T(8,128)(2,1)} custom-call(bf16[128,2048]{1,0:T(8,128)(2,1)} %bitcast.79, bf16[8,448,1024]{2,1,0:T(8,128)(2,1)} %bitcast.76), custom_call_target="tpu_custom_call" | custom-call | flops 939524096 | bytes 7864320 | tf_op jit(solution)/shard_map/wide/pallas_call | solution.py:86
  231.8 4.8 %all-to-all-start.5 = ((bf16[4,448,128]{2,1,0:T(8,128)(2,1)}), bf16[4,448,128]{2,1,0:T(8,128)(2,1)S(1)}, u32[]{:S(2)}, u32[]{:S(2)}) async-start(bf16[4,448,128]{2,1,0:T(8,128)(2,1)} %bitcast.84), calls=%async_computation.5 | async-start | bytes 917504 | tf_op jit(solution)/shard_map/all_to_all | solution.py:40
  237.7 5.2 %all-to-all-done.5 = bf16[4,448,128]{2,1,0:T(8,128)(2,1)S(1)} async-done(((bf16[4,448,128]{2,1,0:T(8,128)(2,1)}), bf16[4,448,128]{2,1,0:T(8,128)(2,1)S(1)}, u32[]{:S(2)}, u32[]{:S(2)}) %all-to-all-start.5) | async-done | bytes 458784 | tf_op jit(solution)/shard_map/all_to_all | solution.py:40
  244.2 4.9 %all-to-all-start.7 = ((bf16[4,2,448,128]{3,2,1,0:T(8,128)(2,1)}), bf16[4,2,448,128]{3,2,1,0:T(8,128)(2,1)S(1)}, u32[]{:S(2)}, u32[]{:S(2)}) async-start(bf16[4,2,448,128]{3,2,1,0:T(8,128)(2,1)} %broadcast_in_dim.67), calls=%async_computation.7 | async-start | bytes 1835008 | tf_op jit(solution)/shard_map/all_to_all | solution.py:40
  249.2 9.4 %all-to-all-done.7.act_ref = bf16[4,2,448,128]{3,2,1,0:T(8,128)(2,1)S(1)} async-done(((bf16[4,2,448,128]{3,2,1,0:T(8,128)(2,1)}), bf16[4,2,448,128]{3,2,1,0:T(8,128)(2,1)S(1)}, u32[]{:S(2)}, u32[]{:S(2)}) %all-to-all-start.7) | async-done | bytes 917536 | tf_op jit(solution)/shard_map/all_to_all | solution.py:40
  259.5 10.1 %branch.1 = bf16[4,8,32,256]{3,2,1,0:T(8,128)(2,1)} custom-call(s32[1]{0:T(128)} %bitcast.place_ref, bf16[4,2,448,128]{3,2,1,0:T(8,128)(2,1)} %copy-done.1, bf16[4,2,448,1024]{3,2,1,0:T(8,128)(2,1)} %bitcast.75, bf16[4,2,448,1024]{3,2,1,0:T(8,128)(2,1)} %bitcast.73, bf16[128,256]{1,0:T(8,128)(2,1)} %bitcast.89), custom_call_target="tpu_custom_call" | custom-call | flops 1879048192 | bytes 14680064 | tf_op jit(solution)/shard_map/branch/pallas_call | solution.py:123
  269.5 20.8 %all_to_all.53 = bf16[32,32,256]{2,1,0:T(8,128)(2,1)S(1)} all-to-all(bf16[32,32,256]{2,1,0:T(8,128)(2,1)} %bitcast.80), channel_id=1, replica_groups={{0,1,2,3,4,5,6,7,64,65,66,67,68,69,70,71,128,129,130,131,132,133,134,13..., dimensions={0} | all-to-all | bytes 1048576 | tf_op jit(solution)/shard_map/all_to_all | solution.py:40
  290.4 8.4 %all_to_all.54 = bf16[4,32,256]{2,1,0:T(8,128)(2,1)S(1)} all-to-all(bf16[4,32,256]{2,1,0:T(8,128)(2,1)S(1)} %bitcast_reduce_fusion), channel_id=1, replica_groups={{0,8,16,24},{1,9,17,25},{2,10,18,26},{3,11,19,27},{4,12,20,28},{5,13,21..., dimensions={0} | all-to-all | bytes 131072 | tf_op jit(solution)/shard_map/all_to_all | solution.py:40
  (68 shorter events, 17.8 us)
Async XLA Ops:
  6.5 2.2 copy-start.5
  6.5 2.3 copy-start.6
  6.5 2.3 copy-start.7
  6.5 201.5 %all-gather.11.cloned.1.call-start = ((), (), s32[]{:S(2)}) async-start(), calls=%async_computation.12 | async-start | bytes 8257536 | tf_op jit(solution)/shard_map/all_gather | solution.py:247
  7.3 206.7 %all-gather.9.cloned.1.call-start = ((), (), s32[]{:S(2)}) async-start(), calls=%async_computation.11 | async-start | bytes 8257536 | tf_op jit(solution)/shard_map/all_gather | solution.py:247
  8.0 217.9 %all-gather.7.cloned.1.call-start = ((), (), s32[]{:S(2)}) async-start(), calls=%async_computation.10 | async-start | bytes 8257536 | tf_op jit(solution)/shard_map/all_gather | solution.py:247
  10.6 68.1 %copy-start.8 = (s32[128]{0:T(128)S(1)}, s32[128]{0:T(128)}, u32[]{:S(2)}) copy-start(s32[128]{0:T(128)} %param.17) | copy-start | bytes 1540
  10.6 68.1 %all-to-all-start = ((bf16[32,280,128]{2,1,0:T(8,128)(2,1)}), bf16[32,280,128]{2,1,0:T(8,128)(2,1)S(1)}, u32[]{:S(2)}, u32[]{:S(2)}) async-start(bf16[32,280,128]{2,1,0:T(8,128)(2,1)} %broadcast_in_dim.56), calls=%async_computation | async-start | bytes 4587520 | tf_op jit(solution)/shard_map/all_to_all | solution.py:40
  78.7 1.8 copy-start
  91.7 17.8 %copy-start.2 = (f32[128,512]{1,0:T(8,128)S(1)}, f32[128,512]{1,0:T(8,128)}, u32[]{:S(2)}) copy-start(f32[128,512]{1,0:T(8,128)} %get-tuple-element.8) | copy-start | bytes 786436
  153.0 25.3 %copy-start.4 = (bf16[4,8192]{1,0:T(4,128)(2,1)S(1)}, bf16[4,8192]{1,0:T(4,128)(2,1)}, u32[]{:S(2)}) copy-start(bf16[4,8192]{1,0:T(4,128)(2,1)} %param.10) | copy-start | bytes 196612
  179.2 21.7 %all-to-all-start.6 = ((bf16[32,64,128]{2,1,0:T(8,128)(2,1)}), bf16[32,64,128]{2,1,0:T(8,128)(2,1)S(1)}, u32[]{:S(2)}, u32[]{:S(2)}) async-start(bf16[32,64,128]{2,1,0:T(8,128)(2,1)} %bitcast.20), calls=%async_computation.6 | async-start | bytes 1048576 | tf_op jit(solution)/shard_map/all_to_all | solution.py:40
  186.4 21.7 %copy-start.3 = (bf16[4,32,256]{2,1,0:T(8,128)(2,1)}, bf16[4,32,256]{2,1,0:T(8,128)(2,1)S(1)}, u32[]{:S(2)}) copy-start(bf16[4,32,256]{2,1,0:T(8,128)(2,1)S(1)} %bitcast_reduce_fusion.1) | copy-start | bytes 196612
  201.8 23.3 %all-to-all-start.4 = ((bf16[8,128,256]{2,1,0:T(8,128)(2,1)}), bf16[8,128,256]{2,1,0:T(8,128)(2,1)S(1)}, u32[]{:S(2)}, u32[]{:S(2)}) async-start(bf16[8,128,256]{2,1,0:T(8,128)(2,1)} %broadcast_in_dim.64), calls=%async_computation.4 | async-start | bytes 1048576 | tf_op jit(solution)/shard_map/all_to_all | solution.py:40
  221.0 15.7 %collective-permute-start = (bf16[2,448,128]{2,1,0:T(8,128)(2,1)S(1)}, bf16[2,448,128]{2,1,0:T(8,128)(2,1)S(1)}, u32[]{:S(2)}, u32[]{:S(2)}) collective-permute-start(bf16[2,448,128]{2,1,0:T(8,128)(2,1)S(1)} %get-tuple-element.15), channel_id=1, source_target_pairs={{0,64},{32,96},{64,128},{96,160},{128,192},{160,224},{192,0},{224,... | collective-permute-start | bytes 688136 | tf_op jit(solution)/shard_map/ppermute | solution.py:344
  221.8 14.9 %collective-permute-start.1 = (bf16[2,448,128]{2,1,0:T(8,128)(2,1)S(1)}, bf16[2,448,128]{2,1,0:T(8,128)(2,1)S(1)}, u32[]{:S(2)}, u32[]{:S(2)}) collective-permute-start(bf16[2,448,128]{2,1,0:T(8,128)(2,1)S(1)} %get-tuple-element.17), channel_id=1, source_target_pairs={{0,128},{32,160},{64,192},{96,224},{128,0},{160,32},{192,64},{224,... | collective-permute-start | bytes 688136 | tf_op jit(solution)/shard_map/ppermute | solution.py:344
  224.6 12.1 %collective-permute-start.2 = (bf16[2,448,128]{2,1,0:T(8,128)(2,1)S(1)}, bf16[2,448,128]{2,1,0:T(8,128)(2,1)S(1)}, u32[]{:S(2)}, u32[]{:S(2)}) collective-permute-start(bf16[2,448,128]{2,1,0:T(8,128)(2,1)S(1)} %get-tuple-element.16), channel_id=1, source_target_pairs={{0,192},{32,224},{64,0},{96,32},{128,64},{160,96},{192,128},{224,1... | collective-permute-start | bytes 688136 | tf_op jit(solution)/shard_map/ppermute | solution.py:344
  231.8 11.1 %all-to-all-start.5 = ((bf16[4,448,128]{2,1,0:T(8,128)(2,1)}), bf16[4,448,128]{2,1,0:T(8,128)(2,1)S(1)}, u32[]{:S(2)}, u32[]{:S(2)}) async-start(bf16[4,448,128]{2,1,0:T(8,128)(2,1)} %bitcast.84), calls=%async_computation.5 | async-start | bytes 917504 | tf_op jit(solution)/shard_map/all_to_all | solution.py:40
  244.2 14.3 %all-to-all-start.7 = ((bf16[4,2,448,128]{3,2,1,0:T(8,128)(2,1)}), bf16[4,2,448,128]{3,2,1,0:T(8,128)(2,1)S(1)}, u32[]{:S(2)}, u32[]{:S(2)}) async-start(bf16[4,2,448,128]{3,2,1,0:T(8,128)(2,1)} %broadcast_in_dim.67), calls=%async_computation.7 | async-start | bytes 1835008 | tf_op jit(solution)/shard_map/all_to_all | solution.py:40
  258.6 0.9 copy-start.1
Sparse Core Ops, SparseCore 0:
  9.2 72.4 all-gather.10
  83.5 58.5 all-gather.8
  144.0 56.9 all-gather.6

commit v5 on v4

--- a/solution.py
+++ b/solution.py
@@ -19,6 +19,13 @@
     for z in range(NZ)
 ]
 
+Y_TURNS = {
+    step: [
+        (y * NZ + z, (y + step) % NY * NZ + z) for y in range(NY) for z in range(NZ)
+    ]
+    for step in (1, -1)
+}
+LINES = (0, -1, 1, 2)
 X_TURNS = {
     step: [(x * CORES + c, (x + step) % NX * CORES + c) for x in range(NX) for c in range(CORES)]
     for step in range(1, NX)
@@ -28,6 +35,13 @@
     for c in range(CORES)
     for y in range(NY)
 ]
+Y_TURNS = {
+    step: [
+        (y * NZ + z, (y + step) % NY * NZ + z) for y in range(NY) for z in range(NZ)
+    ]
+    for step in (1, -1)
+}
+LINES = (0, -1, 1, 2)
 X_TURNS = {
     step: [(x * CORES + c, (x + step) % NX * CORES + c) for x in range(NX) for c in range(CORES)]
     for step in range(1, NX)
@@ -176,16 +190,20 @@
     )(grad, weight)
 
 
-def score_kernel(
-    blocks_ref, low_ref, high_ref, columns_ref, probs_ref, logits_ref, marks_ref, low_sum, high_sum
-):
+def score_kernel(place_ref, *refs):
+    *block_refs, low_ref, high_ref, columns_ref, probs_ref = refs[:-4]
+    logits_ref, marks_ref, low_sum, high_sum = refs[-4:]
     step = pl.program_id(0)
-    shards, size, lanes = blocks_ref.shape
-    both = 2 * logits_ref.shape[1]
+    both = 2 * logits_ref.shape[2]
+
+    def tile(block_ref, i):
+        shards, _, lanes = block_ref.shape
+        return block_ref[:, i * both : (i + 1) * both].reshape(shards * both, lanes)
+
     rows = jnp.concatenate(
         [
-            blocks_ref[:, i * both : (i + 1) * both].reshape(shards * both, lanes)
-            for i in range(size // both)
+            jnp.concatenate([tile(block_ref, i) for block_ref in block_refs], axis=0)
+            for i in range(block_refs[0].shape[1] // both)
         ],
         axis=1,
     )
@@ -203,16 +221,18 @@
 
     @pl.when(step == pl.num_programs(0) - 1)
     def _():
+        shards = NY * NZ
         low = low_sum[...].reshape(shards, both, -1)
         high = high_sum[...].reshape(shards, both, -1)
-        logits_ref[...] = low[:, : both // 2] + high[:, both // 2 :]
-
-
-def score(blocks, weight, columns, probs):
-    shards = blocks.shape[0]
+        logits = low[:, : both // 2] + high[:, both // 2 :]
+        for i, line in enumerate(LINES):
+            logits_ref[lax.rem(place_ref[0] + line + NY, NY)] = logits[i * NZ : (i + 1) * NZ]
+
+
+def score(place, blocks, weight, columns, probs):
     count, entries = columns.shape
     vocab, width = weight.shape
-    own_rows = count // shards
+    own_rows = count // (NY * NZ)
     steps = 8
     chunk = width // 2 // steps
     size = chunk // 128 * 2 * own_rows
@@ -220,19 +240,20 @@
     return pl.pallas_call(
         score_kernel,
         grid=(steps,),
-        in_specs=[
-            pl.BlockSpec((shards, size, 128), lambda i: (0, i, 0)),
+        in_specs=[pl.BlockSpec(memory_space=pltpu.SMEM)]
+        + [pl.BlockSpec((block.shape[0], size, 128), lambda i: (0, i, 0)) for block in blocks]
+        + [
             pl.BlockSpec((vocab, chunk), lambda i: (0, i)),
             pl.BlockSpec((vocab, chunk), lambda i: (0, i + steps)),
             band,
             band,
         ],
         out_specs=[
-            pl.BlockSpec((shards, own_rows, vocab), lambda i: (0, 0, 0)),
+            pl.BlockSpec((NY, NZ, own_rows, vocab), lambda i: (0, 0, 0, 0)),
             pl.BlockSpec((count // steps, vocab), lambda i: (i, 0)),
         ],
         out_shape=[
-            jax.ShapeDtypeStruct((shards, own_rows, vocab), jnp.float32),
+            jax.ShapeDtypeStruct((NY, NZ, own_rows, vocab), jnp.float32),
             jax.ShapeDtypeStruct((count, vocab), jnp.float32),
         ],
         scratch_shapes=[pltpu.VMEM((2 * count, vocab), jnp.float32)] * 2,
@@ -240,7 +261,7 @@
             flops=2 * count * weight.size, bytes_accessed=2 * weight.size, transcendentals=0
         ),
         name="score",
-    )(blocks, weight, weight, columns, probs)
+    )(place, *blocks, weight, weight, columns, probs)
 
 
 def gather_weight(weight):
@@ -281,7 +302,14 @@
         axis=0,
     )
     size, whole = own_rows * width // 128, packed.shape[0]
-    arrived = exchange(replicate(packed, shards))
+    line = exchange(replicate(packed, NZ), Z_GROUPS)
+    before = lax.ppermute(line, "vocab", Y_TURNS[1])
+    after = lax.ppermute(line, "vocab", Y_TURNS[-1])
+    far = [
+        lax.ppermute(before[: NZ // 2], "vocab", Y_TURNS[1]),
+        lax.ppermute(after[NZ // 2 :], "vocab", Y_TURNS[-1]),
+    ]
+    blocks = [line, before, after] + far
 
     body_tiles = as_tiles(body_input).reshape(NX, 1, -1, 128)
     body_tiles = jnp.broadcast_to(body_tiles, (NX, NZ) + body_tiles.shape[2:])
@@ -290,19 +318,25 @@
     )
     body_rows = from_tiles(body_tiles, own_rows)
     store = (
-        arrived[:, size:whole]
+        jnp.concatenate([block[:, size:whole] for block in blocks])
         .reshape(shards, 3, slots, entries)
         .transpose(0, 2, 1, 3)
         .reshape(shards * slots, 3 * entries)
     )
-    chosen_slot = (
-        tile_slot[:, None] == lax.broadcasted_iota(jnp.int32, (count, shards * slots), 1)
-    ).astype(jnp.bfloat16)
+    held = lax.broadcasted_iota(jnp.int32, (1, shards * slots), 1)
+    line_slots = NZ * slots
+    shift = jnp.zeros_like(held)
+    for i, step in enumerate(LINES):
+        shift = jnp.where(held // line_slots == i, step, shift)
+    store_slot = (place // NZ + shift + NY) % NY * line_slots + held % line_slots
+    chosen_slot = (tile_slot[:, None] == store_slot).astype(jnp.bfloat16)
     found = jnp.dot(chosen_slot, store, preferred_element_type=jnp.float32)
     row_ids = (found[:, :entries] * RADIX + found[:, entries : 2 * entries]).astype(jnp.int32)
     row_probs = found[:, 2 * entries :]
     tail_mass = 1.0 - jnp.sum(row_probs, axis=1, keepdims=True)
-    logits, marks = score(arrived, head_weight, row_ids - place * vocab, row_probs)
+    logits, marks = score(
+        (place // NZ).reshape(1), blocks, head_weight, row_ids - place * vocab, row_probs
+    )
     logits = logits.reshape(count, vocab)
     picked = marks >= 0.0
     teacher = jnp.maximum(marks, 0.0)

time: 309 us -> 306 us (level)
  waiting for transfers between devices: 87.8 us -> 63.3 us
  blocking collectives: 102 us -> 126 us
  starting transfers between devices: 37.2 us -> 32.2 us
    all_to_all x5 -> x4, waiting for transfers between devices: 85.7 us -> 29.2 us  [exchange(): return lax.all_to_all(blocks, axis, 0, 0, axis_index_groups=groups)]
    ppermute x0 -> x4, waiting for transfers between devices: none -> 32 us  [the longest x1 25.2 us: layers(): before = lax.ppermute(line, 'vocab', Y_TURNS[1])]
    all_to_all x5 -> x6, blocking collectives: 102 us -> 126 us  [exchange(): return lax.all_to_all(blocks, axis, 0, 0, axis_index_groups=groups)]
    all_to_all x5 -> x4, starting transfers between devices: 33 us -> 21.4 us  [exchange(): return lax.all_to_all(blocks, axis, 0, 0, axis_index_groups=groups)]
    ppermute x0 -> x4, starting transfers between devices: none -> 6.63 us  [the longest x1 2.98 us: layers(): lax.ppermute(after[NZ // 2:], 'vocab', Y_TURNS[-1])]
  transfers between devices with their start and end apart: 11 -> 14, of which waited for: 4 -> 5; matrix products, arithmetic and copies ran while one was open for 5% -> 6% of each run, Pallas kernels for 12% -> 12%
where the time goes in v5:
time: 306 us; the launch traced here: 302 us
  blocking collectives  126 us (41%)
  waiting for transfers between devices  63.3 us (21%)
  Pallas kernels  47.2 us (15%)
  starting transfers between devices  32.2 us (11%)
  between operations  13.3 us (4%)
  local copies, waits for them, and re-layouts  10.5 us (3%)
  other arithmetic  8.96 us (3%)
    all_to_all x6, blocking collectives, exchange(): return lax.all_to_all(blocks, axis, 0, 0, axis_index_groups=groups)  126 us
    all_to_all x4, waiting for transfers between devices, exchange(): return lax.all_to_all(blocks, axis, 0, 0, axis_index_groups=groups)  29.2 us
    ppermute x1, waiting for transfers between devices, layers(): before = lax.ppermute(line, 'vocab', Y_TURNS[1])  25.2 us
    all_to_all x4, starting transfers between devices, exchange(): return lax.all_to_all(blocks, axis, 0, 0, axis_index_groups=groups)  21.4 us
    pallas_call x3, Pallas kernels, wide(): pl.pallas_call(wide_kernel, grid=(parts,), in_specs=in_specs, out_specs=p...  17.6 us
    pallas_call x1, Pallas kernels, score(): pl.pallas_call(score_kernel, grid=(steps,), in_specs=[pl.BlockSpec(memory...  11.4 us
    pallas_call x1, Pallas kernels, branch_blocks(): pl.pallas_call(branch_kernel, grid=(NZ,), in_specs=[pl.BlockSpec(memory_s...  10 us
    pallas_call x1, Pallas kernels, head_blocks(): pl.pallas_call(head_kernel, grid=(parts // step,), in_specs=[pl.BlockSpec...  8.15 us
  transfers between devices with their start and end apart: 14, of which 5 were waited for; matrix products, arithmetic and copies ran while one was open for 6% of the time, Pallas kernels for 12%

profile of v5, /device:TPU:2, one launch (start us, length us, event | category | flops | bytes accessed | tf_op | source)
XLA Modules:
  0.0 302.1 jit_solution(1922037512690450784)
XLA Ops:
  11.1 26.8 %all_to_all.50.refs_0_ = bf16[8,280,128]{2,1,0:T(8,128)(2,1)S(1)} all-to-all(bf16[8,280,128]{2,1,0:T(8,128)(2,1)S(1)} %broadcast_in_dim.63), channel_id=1, replica_groups={{0,1,2,3,4,5,6,7},{8,9,10,11,12,13,14,15},{16,17,18,19,20,21,22,23},{24..., dimensions={0} | all-to-all | bytes 1146880 | tf_op jit(solution)/shard_map/all_to_all | solution.py:54
  41.2 25.2 %collective-permute-done.refs_1_ = bf16[8,280,128]{2,1,0:T(8,128)(2,1)S(1)} collective-permute-done((bf16[8,280,128]{2,1,0:T(8,128)(2,1)S(1)}, bf16[8,280,128]{2,1,0:T(8,128)(2,1)S(1)}, u32[]{:S(2)}, u32[]{:S(2)}) %collective-permute-start) | collective-permute-done | bytes 573472 | tf_op jit(solution)/shard_map/ppermute | solution.py:306
  66.9 3.0 collective-permute-start.3
  69.9 6.8 %collective-permute-done.2.refs_3_ = bf16[4,280,128]{2,1,0:T(8,128)(2,1)S(1)} collective-permute-done((bf16[4,280,128]{2,1,0:T(8,128)(2,1)S(1)}, bf16[4,280,128]{2,1,0:T(8,128)(2,1)S(1)}, u32[]{:S(2)}, u32[]{:S(2)}) %collective-permute-start.2) | collective-permute-done | bytes 286752 | tf_op jit(solution)/shard_map/ppermute | solution.py:309
  78.9 11.4 %score.1 = (f32[4,8,4,512]{3,2,1,0:T(4,128)}, f32[128,512]{1,0:T(8,128)}) custom-call(s32[1]{0:T(128)} %bitcast.1.place_ref, bf16[8,280,128]{2,1,0:T(8,128)(2,1)} %copy-done.1, bf16[8,280,128]{2,1,0:T(8,128)(2,1)} %copy-done.2, bf16[8,280,128]{2,1,0:T(8,128)(2,1)} %copy-done.3, bf16[4,280,128]{2,1,0:T(8,128)(2,1)} %copy-done.5, ...), custom_call_target="tpu_custom_call" | custom-call | flops 1073741824 | bytes 8388608 | tf_op jit(solution)/shard_map/score/pallas_call | solution.py:240
  94.1 18.6 %all_to_all.51 = f32[32,4,128]{2,1,0:T(4,128)S(1)} all-to-all(f32[32,4,128]{2,1,0:T(4,128)S(1)} %broadcast_in_dim.70), channel_id=1, replica_groups=mesh['dp'=8,'vocab'=32] {'vocab'}, dimensions={0} | all-to-all | bytes 131072 | tf_op jit(solution)/shard_map/all_to_all | solution.py:54
  112.8 1.9 multiply_convert_fusion.grad_ref
  114.7 8.1 %head.1 = bf16[4,32,32,256]{3,2,1,0:T(8,128)(2,1)} custom-call(bf16[128,512]{1,0:T(8,128)(2,1)} %multiply_convert_fusion.grad_ref, bf16[512,8192]{1,0:T(8,128)(2,1)} %weight_ref.1), custom_call_target="tpu_custom_call" | custom-call | flops 1073741824 | bytes 8388608 | tf_op jit(solution)/shard_map/head/pallas_call | solution.py:175
  122.9 28.8 %all_to_all.52 = bf16[4,32,32,256]{3,2,1,0:T(8,128)(2,1)S(1)} all-to-all(bf16[4,32,32,256]{3,2,1,0:T(8,128)(2,1)} %head.1), channel_id=1, replica_groups={{0,8,16,24},{1,9,17,25},{2,10,18,26},{3,11,19,27},{4,12,20,28},{5,13,21..., dimensions={0} | all-to-all | bytes 4194304 | tf_op jit(solution)/shard_map/all_to_all | solution.py:54
  152.1 22.4 %all_to_all.53 = bf16[32,32,256]{2,1,0:T(8,128)(2,1)S(1)} all-to-all(bf16[32,32,256]{2,1,0:T(8,128)(2,1)S(1)} %reduce_sum.97), channel_id=1, replica_groups={{0,1,2,3,4,5,6,7,64,65,66,67,68,69,70,71,128,129,130,131,132,133,134,13..., dimensions={0} | all-to-all | bytes 1048576 | tf_op jit(solution)/shard_map/all_to_all | solution.py:54
  175.4 7.0 %all-to-all-start.6 = ((bf16[32,64,128]{2,1,0:T(8,128)(2,1)}), bf16[32,64,128]{2,1,0:T(8,128)(2,1)S(1)}, u32[]{:S(2)}, u32[]{:S(2)}) async-start(bf16[32,64,128]{2,1,0:T(8,128)(2,1)} %bitcast.21), calls=%async_computation.6 | async-start | bytes 1048576 | tf_op jit(solution)/shard_map/all_to_all | solution.py:54
  182.5 14.6 %all-to-all-done.6 = bf16[32,64,128]{2,1,0:T(8,128)(2,1)S(1)} async-done(((bf16[32,64,128]{2,1,0:T(8,128)(2,1)}), bf16[32,64,128]{2,1,0:T(8,128)(2,1)S(1)}, u32[]{:S(2)}, u32[]{:S(2)}) %all-to-all-start.6) | async-done | bytes 524320 | tf_op jit(solution)/shard_map/all_to_all | solution.py:54
  198.0 4.6 %all-to-all-start.4 = ((bf16[8,128,256]{2,1,0:T(8,128)(2,1)}), bf16[8,128,256]{2,1,0:T(8,128)(2,1)S(1)}, u32[]{:S(2)}, u32[]{:S(2)}) async-start(bf16[8,128,256]{2,1,0:T(8,128)(2,1)} %broadcast_in_dim.72), calls=%async_computation.4 | async-start | bytes 1048576 | tf_op jit(solution)/shard_map/all_to_all | solution.py:54
  204.2 5.9 %wide.4.refs_0_ = bf16[4,2,448,128]{3,2,1,0:T(8,128)(2,1)} custom-call(bf16[128,2048]{1,0:T(8,128)(2,1)} %bitcast.78, bf16[8,448,1024]{2,1,0:T(8,128)(2,1)} %bitcast.75), custom_call_target="tpu_custom_call" | custom-call | flops 939524096 | bytes 7864320 | tf_op jit(solution)/shard_map/wide/pallas_call | solution.py:100
  210.1 5.9 %wide.5 = bf16[4,2,448,128]{3,2,1,0:T(8,128)(2,1)} custom-call(bf16[128,2048]{1,0:T(8,128)(2,1)} %bitcast.79, bf16[8,448,1024]{2,1,0:T(8,128)(2,1)} %bitcast.73, bf16[4,2,448,128]{3,2,1,0:T(8,128)(2,1)} %wide.4.refs_0_), custom_call_target="tpu_custom_call", output_to_operand_aliasing={{}: (2, {})} | custom-call | flops 939524096 | bytes 7864320 | tf_op jit(solution)/shard_map/wide/pallas_call | solution.py:100
  218.0 2.8 collective-permute-start.5
  222.1 5.9 %wide.3 = bf16[4,1,448,128]{3,2,1,0:T(8,128)(2,1)} custom-call(bf16[128,2048]{1,0:T(8,128)(2,1)} %bitcast.80, bf16[8,448,1024]{2,1,0:T(8,128)(2,1)} %bitcast.77), custom_call_target="tpu_custom_call" | custom-call | flops 939524096 | bytes 7864320 | tf_op jit(solution)/shard_map/wide/pallas_call | solution.py:100
  228.0 4.9 %all-to-all-start.5 = ((bf16[4,448,128]{2,1,0:T(8,128)(2,1)}), bf16[4,448,128]{2,1,0:T(8,128)(2,1)S(1)}, u32[]{:S(2)}, u32[]{:S(2)}) async-start(bf16[4,448,128]{2,1,0:T(8,128)(2,1)} %bitcast.85), calls=%async_computation.5 | async-start | bytes 917504 | tf_op jit(solution)/shard_map/all_to_all | solution.py:54
  233.9 5.2 %all-to-all-done.5 = bf16[4,448,128]{2,1,0:T(8,128)(2,1)S(1)} async-done(((bf16[4,448,128]{2,1,0:T(8,128)(2,1)}), bf16[4,448,128]{2,1,0:T(8,128)(2,1)S(1)}, u32[]{:S(2)}, u32[]{:S(2)}) %all-to-all-start.5) | async-done | bytes 458784 | tf_op jit(solution)/shard_map/all_to_all | solution.py:54
  240.4 4.9 %all-to-all-start.7 = ((bf16[4,2,448,128]{3,2,1,0:T(8,128)(2,1)}), bf16[4,2,448,128]{3,2,1,0:T(8,128)(2,1)S(1)}, u32[]{:S(2)}, u32[]{:S(2)}) async-start(bf16[4,2,448,128]{3,2,1,0:T(8,128)(2,1)} %broadcast_in_dim.75), calls=%async_computation.7 | async-start | bytes 1835008 | tf_op jit(solution)/shard_map/all_to_all | solution.py:54
  245.3 9.4 %all-to-all-done.7.act_ref = bf16[4,2,448,128]{3,2,1,0:T(8,128)(2,1)S(1)} async-done(((bf16[4,2,448,128]{3,2,1,0:T(8,128)(2,1)}), bf16[4,2,448,128]{3,2,1,0:T(8,128)(2,1)S(1)}, u32[]{:S(2)}, u32[]{:S(2)}) %all-to-all-start.7) | async-done | bytes 917536 | tf_op jit(solution)/shard_map/all_to_all | solution.py:54
  255.6 10.0 %branch.1 = bf16[4,8,32,256]{3,2,1,0:T(8,128)(2,1)} custom-call(s32[1]{0:T(128)} %bitcast.place_ref, bf16[4,2,448,128]{3,2,1,0:T(8,128)(2,1)} %copy-done, bf16[4,2,448,1024]{3,2,1,0:T(8,128)(2,1)} %bitcast.76, bf16[4,2,448,1024]{3,2,1,0:T(8,128)(2,1)} %bitcast.74, bf16[128,256]{1,0:T(8,128)(2,1)} %bitcast.90), custom_call_target="tpu_custom_call" | custom-call | flops 1879048192 | bytes 14680064 | tf_op jit(solution)/shard_map/branch/pallas_call | solution.py:137
  265.7 20.8 %all_to_all.54 = bf16[32,32,256]{2,1,0:T(8,128)(2,1)S(1)} all-to-all(bf16[32,32,256]{2,1,0:T(8,128)(2,1)} %bitcast.81), channel_id=1, replica_groups={{0,1,2,3,4,5,6,7,64,65,66,67,68,69,70,71,128,129,130,131,132,133,134,13..., dimensions={0} | all-to-all | bytes 1048576 | tf_op jit(solution)/shard_map/all_to_all | solution.py:54
  286.5 8.4 %all_to_all.55 = bf16[4,32,256]{2,1,0:T(8,128)(2,1)S(1)} all-to-all(bf16[4,32,256]{2,1,0:T(8,128)(2,1)S(1)} %bitcast_reduce_fusion), channel_id=1, replica_groups={{0,8,16,24},{1,9,17,25},{2,10,18,26},{3,11,19,27},{4,12,20,28},{5,13,21..., dimensions={0} | all-to-all | bytes 131072 | tf_op jit(solution)/shard_map/all_to_all | solution.py:54
  (81 shorter events, 25.7 us)
Async XLA Ops:
  6.5 197.7 %all-gather.11.cloned.1.call-start = ((), (), s32[]{:S(2)}) async-start(), calls=%async_computation.12 | async-start | bytes 8257536 | tf_op jit(solution)/shard_map/all_gather | solution.py:268
  7.3 202.8 %all-gather.9.cloned.1.call-start = ((), (), s32[]{:S(2)}) async-start(), calls=%async_computation.11 | async-start | bytes 8257536 | tf_op jit(solution)/shard_map/all_gather | solution.py:268
  8.0 214.1 %all-gather.7.cloned.1.call-start = ((), (), s32[]{:S(2)}) async-start(), calls=%async_computation.10 | async-start | bytes 8257536 | tf_op jit(solution)/shard_map/all_gather | solution.py:268
  37.9 41.0 %copy-start.1 = (bf16[8,280,128]{2,1,0:T(8,128)(2,1)}, bf16[8,280,128]{2,1,0:T(8,128)(2,1)S(1)}, u32[]{:S(2)}) copy-start(bf16[8,280,128]{2,1,0:T(8,128)(2,1)S(1)} %all_to_all.50.refs_0_) | copy-start | bytes 1720324
  37.9 28.5 %collective-permute-start = (bf16[8,280,128]{2,1,0:T(8,128)(2,1)S(1)}, bf16[8,280,128]{2,1,0:T(8,128)(2,1)S(1)}, u32[]{:S(2)}, u32[]{:S(2)}) collective-permute-start(bf16[8,280,128]{2,1,0:T(8,128)(2,1)S(1)} %all_to_all.50.refs_0_), channel_id=1, source_target_pairs={{0,8},{1,9},{2,10},{3,11},{4,12},{5,13},{6,14},{7,15},{8,16},{9,17... | collective-permute-start | bytes 1720328 | tf_op jit(solution)/shard_map/ppermute | solution.py:306
  39.5 27.3 %collective-permute-start.1 = (bf16[8,280,128]{2,1,0:T(8,128)(2,1)S(1)}, bf16[8,280,128]{2,1,0:T(8,128)(2,1)S(1)}, u32[]{:S(2)}, u32[]{:S(2)}) collective-permute-start(bf16[8,280,128]{2,1,0:T(8,128)(2,1)S(1)} %all_to_all.50.refs_0_), channel_id=1, source_target_pairs={{0,24},{1,25},{2,26},{3,27},{4,28},{5,29},{6,30},{7,31},{8,0},{9,1... | collective-permute-start | bytes 1720328 | tf_op jit(solution)/shard_map/ppermute | solution.py:307
  66.4 12.5 %copy-start.2 = (bf16[8,280,128]{2,1,0:T(8,128)(2,1)}, bf16[8,280,128]{2,1,0:T(8,128)(2,1)S(1)}, u32[]{:S(2)}) copy-start(bf16[8,280,128]{2,1,0:T(8,128)(2,1)S(1)} %collective-permute-done.refs_1_) | copy-start | bytes 1720324
  66.4 10.2 %collective-permute-start.2 = (bf16[4,280,128]{2,1,0:T(8,128)(2,1)S(1)}, bf16[4,280,128]{2,1,0:T(8,128)(2,1)S(1)}, u32[]{:S(2)}, u32[]{:S(2)}) collective-permute-start(bf16[4,280,128]{2,1,0:T(8,128)(2,1)S(1)} %slice.40), channel_id=1, source_target_pairs={{0,8},{1,9},{2,10},{3,11},{4,12},{5,13},{6,14},{7,15},{8,16},{9,17... | collective-permute-start | bytes 860168 | tf_op jit(solution)/shard_map/ppermute | solution.py:309
  66.8 12.1 %copy-start.3 = (bf16[8,280,128]{2,1,0:T(8,128)(2,1)}, bf16[8,280,128]{2,1,0:T(8,128)(2,1)S(1)}, u32[]{:S(2)}) copy-start(bf16[8,280,128]{2,1,0:T(8,128)(2,1)S(1)} %collective-permute-done.1.refs_2_) | copy-start | bytes 1720324
  66.9 9.8 %collective-permute-start.3 = (bf16[4,280,128]{2,1,0:T(8,128)(2,1)S(1)}, bf16[4,280,128]{2,1,0:T(8,128)(2,1)S(1)}, u32[]{:S(2)}, u32[]{:S(2)}) collective-permute-start(bf16[4,280,128]{2,1,0:T(8,128)(2,1)S(1)} %slice.41), channel_id=1, source_target_pairs={{0,24},{1,25},{2,26},{3,27},{4,28},{5,29},{6,30},{7,31},{8,0},{9,1... | collective-permute-start | bytes 860168 | tf_op jit(solution)/shard_map/ppermute | solution.py:310
  76.6 2.3 copy-start.5
  76.7 2.2 copy-start.6
  114.7 59.8 %copy-start.7 = (bf16[4,8192]{1,0:T(4,128)(2,1)S(1)}, bf16[4,8192]{1,0:T(4,128)(2,1)}, u32[]{:S(2)}) copy-start(bf16[4,8192]{1,0:T(4,128)(2,1)} %param.10) | copy-start | bytes 196612
  175.4 21.7 %all-to-all-start.6 = ((bf16[32,64,128]{2,1,0:T(8,128)(2,1)}), bf16[32,64,128]{2,1,0:T(8,128)(2,1)S(1)}, u32[]{:S(2)}, u32[]{:S(2)}) async-start(bf16[32,64,128]{2,1,0:T(8,128)(2,1)} %bitcast.21), calls=%async_computation.6 | async-start | bytes 1048576 | tf_op jit(solution)/shard_map/all_to_all | solution.py:54
  182.5 33.4 %copy-start.4 = (bf16[4,32,256]{2,1,0:T(8,128)(2,1)}, bf16[4,32,256]{2,1,0:T(8,128)(2,1)S(1)}, u32[]{:S(2)}) copy-start(bf16[4,32,256]{2,1,0:T(8,128)(2,1)S(1)} %bitcast_reduce_fusion.1) | copy-start | bytes 196612
  198.0 23.3 %all-to-all-start.4 = ((bf16[8,128,256]{2,1,0:T(8,128)(2,1)}), bf16[8,128,256]{2,1,0:T(8,128)(2,1)S(1)}, u32[]{:S(2)}, u32[]{:S(2)}) async-start(bf16[8,128,256]{2,1,0:T(8,128)(2,1)} %broadcast_in_dim.72), calls=%async_computation.4 | async-start | bytes 1048576 | tf_op jit(solution)/shard_map/all_to_all | solution.py:54
  217.1 15.7 %collective-permute-start.4 = (bf16[2,448,128]{2,1,0:T(8,128)(2,1)S(1)}, bf16[2,448,128]{2,1,0:T(8,128)(2,1)S(1)}, u32[]{:S(2)}, u32[]{:S(2)}) collective-permute-start(bf16[2,448,128]{2,1,0:T(8,128)(2,1)S(1)} %get-tuple-element.15), channel_id=1, source_target_pairs={{0,64},{32,96},{64,128},{96,160},{128,192},{160,224},{192,0},{224,... | collective-permute-start | bytes 688136 | tf_op jit(solution)/shard_map/ppermute | solution.py:378
  218.0 14.9 %collective-permute-start.5 = (bf16[2,448,128]{2,1,0:T(8,128)(2,1)S(1)}, bf16[2,448,128]{2,1,0:T(8,128)(2,1)S(1)}, u32[]{:S(2)}, u32[]{:S(2)}) collective-permute-start(bf16[2,448,128]{2,1,0:T(8,128)(2,1)S(1)} %get-tuple-element.17), channel_id=1, source_target_pairs={{0,128},{32,160},{64,192},{96,224},{128,0},{160,32},{192,64},{224,... | collective-permute-start | bytes 688136 | tf_op jit(solution)/shard_map/ppermute | solution.py:378
  220.7 12.1 %collective-permute-start.6 = (bf16[2,448,128]{2,1,0:T(8,128)(2,1)S(1)}, bf16[2,448,128]{2,1,0:T(8,128)(2,1)S(1)}, u32[]{:S(2)}, u32[]{:S(2)}) collective-permute-start(bf16[2,448,128]{2,1,0:T(8,128)(2,1)S(1)} %get-tuple-element.16), channel_id=1, source_target_pairs={{0,192},{32,224},{64,0},{96,32},{128,64},{160,96},{192,128},{224,1... | collective-permute-start | bytes 688136 | tf_op jit(solution)/shard_map/ppermute | solution.py:378
  228.0 11.1 %all-to-all-start.5 = ((bf16[4,448,128]{2,1,0:T(8,128)(2,1)}), bf16[4,448,128]{2,1,0:T(8,128)(2,1)S(1)}, u32[]{:S(2)}, u32[]{:S(2)}) async-start(bf16[4,448,128]{2,1,0:T(8,128)(2,1)} %bitcast.85), calls=%async_computation.5 | async-start | bytes 917504 | tf_op jit(solution)/shard_map/all_to_all | solution.py:54
  240.4 14.3 %all-to-all-start.7 = ((bf16[4,2,448,128]{3,2,1,0:T(8,128)(2,1)}), bf16[4,2,448,128]{3,2,1,0:T(8,128)(2,1)S(1)}, u32[]{:S(2)}, u32[]{:S(2)}) async-start(bf16[4,2,448,128]{3,2,1,0:T(8,128)(2,1)} %broadcast_in_dim.75), calls=%async_computation.7 | async-start | bytes 1835008 | tf_op jit(solution)/shard_map/all_to_all | solution.py:54
  254.7 0.9 copy-start
Sparse Core Ops, SparseCore 0:
  9.2 64.8 all-gather.10
  75.9 52.4 all-gather.8
  130.2 52.0 all-gather.6
